TPU v7x, 32 devices: a whole 2x2x4 slice. The times are simulated.
32 devices in a mesh: lat: 4 (over y, x), lon: 8 (over z, core).
Axes of the slice: x: 2, y: 2, z: 4, core: 2. Of those that a mesh axis runs over, the one named last changes fastest.
Arguments:
- fields: bfloat16 [16, 720, 641], P('lat', 'lon'), may hold values from -36 to 36
- group_size: int32 [8], replicated, may hold values from 1 to 121, 641 in all
- band_of_row: int32 [16], P('lat'), may hold values from 0 to 7, never falling along the last dimension, each value on 1 to 4 neighbouring positions
- basis_spectra: float32 [8, 9, 8, 2, 361], replicated, may hold values from -0.75 to 0.75
- basis_coef: float32 [641, 8], replicated, may hold values from -5 to 5
- mlp_gain: float32 [641], replicated, may hold values from 0.25 to 1.75
- w_in: bfloat16 [641, 1282], replicated, may hold values from -0.25 to 0.25
- w_out: bfloat16 [1282, 641], replicated, may hold values from -0.15625 to 0.15625
Outputs:
- block_out: bfloat16 [16, 720, 641], P('lat', 'lon')
Inputs may be any that keep to these rules, and one draw needn't show every extreme that they name: `group_size`: group j holds the channels that follow those of groups 0 to j - 1; the sizes sum to 641. `band_of_row`: band numbers never fall along latitude; every band covers 1 to 4 rows.
All inputs are finite; a program needn't handle non-finite values.
Results may differ from a plain program's by a relative error of at most 0.0051.
Values may be sent and summed in bfloat16 or wider, within the bound.
A program may use at most 64 MiB of HBM per device.

v0:
```python
import math

import jax
import jax.numpy as jnp
from jax import lax
from jax.sharding import PartitionSpec as P

HALO = 4


EPSILON = 1e-05


def padded(cells, sides, width):
    for axis, dim in sides:
        count = lax.axis_size(axis)
        ends = count - 1
        head = lax.slice_in_dim(cells, 0, width, axis=dim)
        tail = lax.slice_in_dim(cells, cells.shape[dim] - width, cells.shape[dim], axis=dim)
        cells = jnp.concatenate(
            [
                lax.ppermute(tail, axis, [(i, (i + 1) % count) for i in range(ends)]),
                cells,
                lax.ppermute(head, axis, [((i + 1) % count, i) for i in range(ends)]),
            ],
            axis=dim,
        )
    return cells


def to_groups(block, send_index, group_count, slot_count):
    row_count = block.shape[0]
    col_count = block.shape[1]
    packed = jnp.take(block, send_index, axis=2).reshape(
        row_count, col_count, group_count, slot_count
    )
    packed = jnp.transpose(packed, (0, 2, 3, 1)).reshape(
        row_count, group_count, slot_count * col_count
    )
    arrived = lax.all_to_all(packed, "lon", split_axis=1, concat_axis=1, tiled=True)
    return arrived.reshape(row_count, group_count, slot_count, col_count)


def normalize(grouped, slot_mask, count):
    values = grouped.astype(jnp.float32)
    weight = slot_mask[None, None, :, None]
    centre = jnp.sum(values * weight, axis=(1, 2, 3)) / count
    centred = values - centre[:, None, None, None]
    spread = jnp.sum(centred * centred * weight, axis=(1, 2, 3)) / count
    return centred * lax.rsqrt(spread + EPSILON)[:, None, None, None]


def forward(normed, forward_table):
    return jnp.einsum("rngc,ncpk->rgpk", normed, forward_table, precision=lax.Precision.HIGHEST)


def per_device(fields, group_size, band_of_row, basis_spectra, basis_coef, mlp_gain, w_in, w_out):
    row_count, col_count, chan_count = fields.shape
    group_count = lax.axis_size("lon")
    lon_count = col_count * group_count
    slot_count = 3 * chan_count // (2 * group_count) + 1
    freq_count = lon_count // 2 + 1
    taps = 2 * HALO + 1
    my_index = lax.axis_index("lon")
    starts = jnp.cumsum(group_size) - group_size
    my_start = starts[my_index]
    my_size = group_size[my_index]
    slots = jnp.arange(slot_count, dtype=jnp.int32)
    channel = jnp.arange(chan_count, dtype=jnp.int32)
    send_index = jnp.minimum(starts[:, None] + slots[None, :], chan_count - 1).reshape(-1)
    group_of = jnp.sum((channel[:, None] >= starts[None, :]).astype(jnp.int32), axis=1) - 1
    back_index = group_of * slot_count + channel - starts[group_of]
    slot_mask = (slots < my_size).astype(jnp.float32)
    count = my_size.astype(jnp.float32) * lon_count
    freq_index = jnp.arange(freq_count, dtype=jnp.int32)
    lon_index = jnp.arange(lon_count, dtype=jnp.int32)
    phase = freq_index[:, None] * lon_index[None, :] % lon_count
    angle = phase.astype(jnp.float32) * (2.0 * math.pi / lon_count)
    cosine = jnp.cos(angle)
    sine = jnp.where(2 * phase % lon_count == 0, 0.0, jnp.sin(angle))
    forward_table = jnp.stack([cosine.T, -sine.T], axis=1).reshape(
        group_count, col_count, 2, freq_count
    )
    edge = (freq_index == 0) | (2 * freq_index == lon_count)
    inv_weight = (jnp.where(edge, 1.0, 2.0) / lon_count)[:, None]
    inverse_table = jnp.stack([cosine * inv_weight, -sine * inv_weight], axis=0).reshape(
        2, freq_count, group_count, col_count
    )
    own = to_groups(fields, send_index, group_count, slot_count)
    widened = padded(own, (("lat", 0),), HALO)
    spectrum = forward(normalize(widened, slot_mask, count), forward_table)
    band_count = basis_spectra.shape[0]
    basis_count = basis_spectra.shape[2]
    band_onehot = (band_of_row[:, None] == jnp.arange(band_count, dtype=jnp.int32)[None, :]).astype(
        jnp.float32
    )
    row_basis = jnp.dot(
        band_onehot, basis_spectra.reshape(band_count, -1), precision=lax.Precision.HIGHEST
    )
    row_basis = row_basis.reshape(row_count, taps, basis_count, 2, freq_count)
    slot_chan = jnp.minimum(my_start + slots, chan_count - 1)
    slot_onehot = (slot_chan[:, None] == channel[None, :]).astype(jnp.float32)
    slot_coef = jnp.dot(slot_onehot, basis_coef, precision=lax.Precision.HIGHEST)
    kernel = jnp.einsum("gb,rdbpk->rdgpk", slot_coef, row_basis, precision=lax.Precision.HIGHEST)
    prod_real = jnp.zeros((row_count, slot_count, freq_count), jnp.float32)
    prod_imag = jnp.zeros((row_count, slot_count, freq_count), jnp.float32)
    for offset in range(taps):
        window = spectrum[offset : offset + row_count]
        kern_real = kernel[:, offset, :, 0]
        kern_imag = kernel[:, offset, :, 1]
        prod_real = prod_real + kern_real * window[:, :, 0] - kern_imag * window[:, :, 1]
        prod_imag = prod_imag + kern_real * window[:, :, 1] + kern_imag * window[:, :, 0]
    product = jnp.stack([prod_real, prod_imag], axis=2)
    corr = jnp.einsum("rgpk,pknc->rngc", product, inverse_table, precision=lax.Precision.HIGHEST)
    mixed_groups = (own.astype(jnp.float32) + corr).astype(jnp.bfloat16)
    outgoing = mixed_groups.reshape(row_count, group_count, slot_count * col_count)
    returned = lax.all_to_all(outgoing, "lon", split_axis=1, concat_axis=1, tiled=True)
    returned = returned.reshape(row_count, group_count * slot_count, col_count)
    mixed = jnp.swapaxes(jnp.take(returned, back_index, axis=1), 1, 2)
    inputs = mixed.reshape(row_count * col_count, chan_count).astype(jnp.float32)
    centre = jnp.mean(inputs, axis=-1, keepdims=True)
    spread = jnp.mean((inputs - centre) ** 2, axis=-1, keepdims=True)
    normalised = ((inputs - centre) * lax.rsqrt(spread + EPSILON) * mlp_gain).astype(jnp.bfloat16)
    hidden = jax.nn.gelu(
        jnp.dot(normalised, w_in, preferred_element_type=jnp.float32), approximate=False
    ).astype(jnp.bfloat16)
    result = inputs + jnp.dot(hidden, w_out, preferred_element_type=jnp.float32)
    return result.astype(jnp.bfloat16).reshape(row_count, col_count, chan_count)


def solution(mesh):
    placed = (P("lat", "lon", None), P(), P("lat"), P(), P(), P(), P(), P())
    return jax.shard_map(
        per_device, mesh=mesh, in_specs=placed, out_specs=P("lat", "lon", None), check_vma=False
    )
```

profile of v0, /device:TPU:0, one launch (start us, length us, event | category | flops | bytes accessed | tf_op | source)
XLA Modules:
  0.0 186.6 jit_solution(5616219020420983903)
XLA Ops:
  0.0 1.0 reduce-window.9
  1.0 0.7 bitcast_subtract_fusion
  1.9 1.8 copy.260
  3.7 7.5 %gather_fusion = bf16[968,4,90]{2,1,0:T(4,128)(2,1)} fusion(bf16[4,90,641]{1,0,2:T(4,128)(2,1)S(1)} %copy.260, s32[1024]{0:T(1024)S(1)} %pad_clamp_fusion.1), kind=kCustom, calls=%fused_computation | custom fusion | bytes 1397792 | tf_op jit(solution)/shard_map/jit(_take)/gather | solution.py:34
  11.2 1.4 fusion.52
  12.7 2.4 %reshape.468 = bf16[4,8,10890]{2,1,0:T(8,128)(2,1)} reshape(bf16[4,8,121,90]{3,2,1,0:T(8,128)(2,1)S(1)} %fusion.52) | data formatting | bytes 1393920 | tf_op jit(solution)/shard_map/reshape | solution.py:37
  15.0 2.2 %copy.262 = bf16[4,8,10890]{2,0,1:T(4,128)(2,1)} copy(bf16[4,8,10890]{2,1,0:T(8,128)(2,1)} %reshape.468) | data formatting | bytes 1393920 | tf_op jit(solution)/shard_map/reshape | solution.py:37
  17.2 6.9 %all-to-all-start = ((bf16[4,8,10890]{2,0,1:T(4,128)(2,1)}), bf16[4,8,10890]{2,0,1:T(4,128)(2,1)}, u32[]{:S(2)}, u32[]{:S(2)}) async-start(bf16[4,8,10890]{2,0,1:T(4,128)(2,1)} %copy.262), calls=%async_computation | async-start | bytes 1409024 | tf_op jit(solution)/shard_map/all_to_all | solution.py:40
  24.2 0.7 fusion.132
  24.9 0.6 add_minimum_fusion.1
  26.8 3.2 %reshape.470 = f32[8,51984]{1,0:T(8,128)S(1)} reshape(f32[8,9,8,2,361]{4,3,2,1,0:T(2,128)} %param.11) | data formatting | bytes 3326976 | tf_op jit(solution)/shard_map/reshape | solution.py:98
  30.0 3.5 %dot_general.26 = f32[9,8,2,361,8]{3,2,1,0,4:T(2,128)} reshape(f32[51984,8]{0,1:T(8,128)S(1)} %bitcast.244) | data formatting | bytes 3326976 | tf_op jit(solution)/shard_map/dot_general | solution.py:97
  33.9 7.2 %fusion.41 = (f32[8,90,1,361]{3,1,0,2:T(8,128)}, f32[8,90,1,361]{3,1,0,2:T(8,128)}) fusion(s32[8,90]{1,0:T(8,128)S(1)} %multiply_add_fusion.1), kind=kLoop, calls=%fused_computation.66 | loop fusion | flops 4938480 | bytes 2082240 | tf_op jit(solution)/shard_map/cos | solution.py:79
  41.1 7.3 %cosine_multiply_fusion = (f32[1,361,8,90]{1,3,0,2:T(8,128)}, f32[1,361,8,90]{1,3,0,2:T(8,128)}) fusion(f32[361]{0:T(512)S(1)} %select_multiply_fusion, s32[8,90]{1,0:T(8,128)S(1)} %multiply_add_fusion.1), kind=kLoop, calls=%fused_computation.71 | loop fusion | flops 5458320 | bytes 2083684 | tf_op jit(solution)/shard_map/mul | solution.py:86
  48.3 2.3 %fusion.28 = f32[4,9,8,2,361]{4,0,3,2,1:T(4,128)} fusion(f32[9,8,2,361,8]{3,2,1,0,4:T(2,128)S(1)} %copy-done.5, s32[4]{0:T(128)S(1)} %copy-done.12), kind=kOutput, calls=%fused_computation.42 | convolution fusion | flops 19961888 | bytes 2495248 | tf_op jit(solution)/shard_map/dot_general | solution.py:97
  50.6 2.0 %copy.263 = bf16[4,8,10890]{2,1,0:T(8,128)(2,1)} copy(bf16[4,8,10890]{2,0,1:T(4,128)(2,1)} %all-to-all-done) | data formatting | bytes 1393920 | tf_op jit(solution)/shard_map/all_to_all | solution.py:40
  52.7 4.5 %reshape.469 = bf16[4,8,121,90]{3,2,1,0:T(8,128)(2,1)S(1)} reshape(bf16[4,8,10890]{2,1,0:T(8,128)(2,1)} %copy.263) | data formatting | bytes 1393920 | tf_op jit(solution)/shard_map/reshape | solution.py:41
  57.2 1.5 copy.264
  58.7 4.3 %collective-permute-start = (bf16[4,8,121,90]{2,1,3,0:T(8,128)(2,1)}, bf16[4,8,121,90]{2,1,3,0:T(8,128)(2,1)}, u32[]{:S(2)}, u32[]{:S(2)}) collective-permute-start(bf16[4,8,121,90]{2,1,3,0:T(8,128)(2,1)} %copy.264), channel_id=1, source_target_pairs={{0,8},{8,16},{16,24},{1,9},{9,17},{17,25},{2,10},{10,18},{18,26},{... | collective-permute-start | bytes 2090888 | tf_op jit(solution)/shard_map/ppermute | solution.py:22
  62.9 1.5 collective-permute-start.1
  64.4 0.6 compare_convert_fusion
  65.0 24.8 %convolution_bitcast_fusion = f32[4,9,121,2,361]{2,4,3,1,0:T(8,128)} fusion(f32[121,8,1,1,1]{0,1,4,3,2:T(8,128)S(1)} %convolution_bitcast_fusion.1, f32[4,9,8,2,361]{4,0,3,2,1:T(4,128)} %fusion.28), kind=kOutput, calls=%fused_computation.6 | convolution fusion | flops 301923072 | bytes 13415744 | tf_op jit(solution)/shard_map/gb,rdbpk->rdgpk/dot_general | solution.py:104
  89.8 2.4 %copy.270 = bf16[4,8,121,90]{3,2,1,0:T(8,128)(2,1)} copy(bf16[4,8,121,90]{2,1,3,0:T(8,128)(2,1)} %collective-permute-done) | data formatting | bytes 1393920 | tf_op jit(solution)/shard_map/ppermute | solution.py:22
  92.2 4.3 %collective-permute-done.1 = bf16[4,8,121,90]{2,1,3,0:T(8,128)(2,1)} collective-permute-done((bf16[4,8,121,90]{2,1,3,0:T(8,128)(2,1)}, bf16[4,8,121,90]{2,1,3,0:T(8,128)(2,1)}, u32[]{:S(2)}, u32[]{:S(2)}) %collective-permute-start.1) | collective-permute-done | bytes 696992 | tf_op jit(solution)/shard_map/ppermute | solution.py:24
  96.5 2.5 %copy.271 = bf16[4,8,121,90]{3,2,1,0:T(8,128)(2,1)} copy(bf16[4,8,121,90]{2,1,3,0:T(8,128)(2,1)} %collective-permute-done.1) | data formatting | bytes 1393920 | tf_op jit(solution)/shard_map/ppermute | solution.py:24
  99.0 3.0 %fusion.7 = f32[12]{0:T(128)S(1)} fusion(f32[121]{0:T(128)S(1)} %compare_convert_fusion, bf16[4,8,121,90]{3,2,1,0:T(8,128)(2,1)} %copy.271, bf16[4,8,121,90]{3,2,1,0:T(8,128)(2,1)} %copy-done.1, bf16[4,8,121,90]{3,2,1,0:T(8,128)(2,1)} %copy.270), kind=kLoop, calls=%fused_computation.11 | loop fusion | flops 5227188 | bytes 2091412 | tf_op jit(solution)/shard_map/reduce_sum | solution.py:47
  102.1 1.9 %fusion.3 = f32[12]{0:T(128)S(1)} fusion(f32[12]{0:T(128)S(1)} %broadcast_divide_fusion, f32[121]{0:T(128)S(1)} %compare_convert_fusion, bf16[4,8,121,90]{3,2,1,0:T(8,128)(2,1)S(1)} %copy-done.4, bf16[4,8,121,90]{3,2,1,0:T(8,128)(2,1)S(1)} %copy-done.2, bf16[4,8,121,90]{3,2,1,0:T(8,128)(2,1)S(1)} %copy-done.3), kind=kLoop, calls=%fused_computation.8 | loop fusion | flops 7318068 | bytes 2091460 | tf_op jit(solution)/shard_map/reduce_sum | solution.py:49
  104.1 18.7 %fusion.15 = f32[12,121,2,361]{1,3,0,2:T(8,128)S(1)} fusion(f32[8,90,1,361]{3,1,0,2:T(8,128)S(1)} %copy-done.11, f32[8,90,1,361]{3,1,0,2:T(8,128)S(1)} %copy-done.10, f32[12]{0:T(128)S(1)} %add_rsqrt_fusion.1, f32[12]{0:T(128)S(1)} %broadcast_divide_fusion, bf16[4,8,121,90]{3,2,1,0:T(8,128)(2,1)S(1)} %copy-done.4, ...), kind=kOutput, calls=%fused_computation.23 | convolution fusion | flops 9066574848 | bytes 8363712 | tf_op jit(solution)/shard_map/rngc,ncpk->rgpk/dot_general | solution.py:54
  122.9 1.8 multiply_subtract_fusion
  124.7 2.3 %multiply_add_fusion = f32[4,121,1,361]{1,3,0,2:T(8,128)S(1)} fusion(f32[4,9,121,2,361]{2,4,3,1,0:T(8,128)S(1)} %bitcast.243, f32[12,121,2,361]{1,3,0,2:T(8,128)S(1)} %fusion.15), kind=kLoop, calls=%fused_computation.134 | loop fusion | flops 6115340 | bytes 25859152 | tf_op jit(solution)/shard_map/add | solution.py:112
  127.0 4.1 %fusion.32 = f32[8,90,4,121]{3,1,2,0:T(8,128)S(1)} fusion(f32[1,361,8,90]{1,3,0,2:T(8,128)S(1)} %copy-done.7, f32[1,361,8,90]{1,3,0,2:T(8,128)S(1)} %copy-done.6, f32[4,121,1,361]{1,3,0,2:T(8,128)S(1)} %multiply_add_fusion, f32[4,121,1,361]{1,3,0,2:T(8,128)S(1)} %multiply_subtract_fusion), kind=kOutput, calls=%fused_computation.51 | convolution fusion | flops 3020100096 | bytes 4871072 | tf_op jit(solution)/shard_map/rgpk,pknc->rngc/dot_general | solution.py:114
  131.1 1.7 fusion.35
  132.8 1.7 copy.343
  134.6 3.7 %reshape.543 = bf16[4,8,10890]{2,0,1:T(4,128)(2,1)} reshape(bf16[4,8,121,90]{3,2,0,1:T(8,128)(2,1)S(1)} %copy.343) | data formatting | bytes 1393920 | tf_op jit(solution)/shard_map/reshape | solution.py:116
  138.3 4.7 %all-to-all-start.1 = ((bf16[4,8,10890]{2,0,1:T(4,128)(2,1)}), bf16[4,8,10890]{2,0,1:T(4,128)(2,1)S(1)}, u32[]{:S(2)}, u32[]{:S(2)}) async-start(bf16[4,8,10890]{2,0,1:T(4,128)(2,1)} %reshape.543), calls=%async_computation.1 | async-start | bytes 1409024 | tf_op jit(solution)/shard_map/all_to_all | solution.py:117
  143.1 4.4 %fusion.93 = (s32[641]{0:T(1024)S(1)}, s32[641,1]{0,1:T(1,128)S(1)}) fusion(s32[]{:T(128)} %bitcast.3, s32[]{:T(128)} %bitcast.4, s32[]{:T(128)} %bitcast.5, s32[]{:T(128)} %bitcast.6, s32[]{:T(128)} %bitcast.7, s32[]{:T(128)} %bitcast.9, s32[]{:T(128)} %bitcast.8, s32[641]{0:T(1024)S(1)} %get-tuple-element.14, s32[641]{0:T(1024)S(1)} %get-tuple-element.13), kind=kLoop, calls=%fused_computation.164 | loop fusion | flops 8974 | bytes 10284 | tf_op jit(solution)/shard_map/gather | solution.py:72
  147.5 0.7 compare_and_fusion.1
  148.2 14.0 %all-to-all-done.1 = bf16[4,8,10890]{2,0,1:T(4,128)(2,1)S(1)} async-done(((bf16[4,8,10890]{2,0,1:T(4,128)(2,1)}), bf16[4,8,10890]{2,0,1:T(4,128)(2,1)S(1)}, u32[]{:S(2)}, u32[]{:S(2)}) %all-to-all-start.1) | async-done | bytes 696992 | tf_op jit(solution)/shard_map/all_to_all | solution.py:117
  162.2 1.4 reshape.472
  163.7 1.3 copy.312
  165.0 2.9 %gather_fusion.1 = bf16[641,4,90]{2,1,0:T(4,128)(2,1)S(1)} fusion(bf16[4,968,90]{2,0,1:T(4,128)(2,1)} %copy.312, s32[1024]{0:T(1024)S(1)} %pad_clamp_fusion), kind=kCustom, calls=%fused_computation.1 | custom fusion | bytes 925604 | tf_op jit(solution)/shard_map/jit(_take)/gather | solution.py:119
  168.0 2.6 %fusion.84 = (f32[4,90]{1,0:T(4,128)S(1)}, bf16[641,4,90]{2,1,0:T(4,128)(2,1)S(1)}) fusion(bf16[641,4,90]{2,1,0:T(4,128)(2,1)S(1)} %gather_fusion.1, pred[641]{0:T(1024)(128)(4,1)S(1)} %get-tuple-element.7), kind=kLoop, calls=%fused_computation.136 | loop fusion | flops 691920 | bytes 925121 | tf_op jit(solution)/shard_map/reduce_sum | solution.py:121
  170.7 0.7 multiply_reduce_fusion
  171.6 1.7 reshape.544
  173.3 2.7 %copy.344 = f32[360,641]{1,0:T(8,128)} copy(f32[360,641]{0,1:T(8,128)} %reshape.544) | data formatting | bytes 1846080 | tf_op jit(solution)/shard_map/convert_element_type | solution.py:120
  176.0 8.1 %fusion.36 = bf16[360,641]{0,1:T(8,128)(2,1)S(1)} fusion(f32[360,641]{0,1:T(8,128)S(1)} %copy-done.8, bf16[1282,641]{0,1:T(8,128)(2,1)S(1)} %copy-done, bf16[641,1282]{1,0:T(8,128)(2,1)} %param.14, f32[360,641]{1,0:T(8,128)} %copy.344, f32[641]{0:T(1024)S(1)} %copy-done.14, f32[360]{0:T(512)S(1)} %rsqrt.20, f32[360]{0:T(512)S(1)} %div.40), kind=kOutput, calls=%fused_computation.57 | convolution fusion | flops 1214719488 | bytes 5600092 | tf_op jit(solution)/shard_map/dot_general | solution.py:127
  184.1 0.8 reshape.545
  184.9 1.6 copy.316
  (65 shorter events, 1.8 us)
Async XLA Ops:
  0.0 175.9 %copy-start = (bf16[1282,641]{0,1:T(8,128)(2,1)S(1)}, bf16[1282,641]{0,1:T(8,128)(2,1)}, u32[]{:S(2)}) copy-start(bf16[1282,641]{0,1:T(8,128)(2,1)} %param.15) | copy-start | bytes 4930576
  12.6 12.9 %copy-start.15 = (s32[8]{0:T(128)S(1)}, s32[8]{0:T(128)}, u32[]{:S(2)}) copy-start(s32[8]{0:T(128)} %param.9) | copy-start | bytes 100
  17.2 33.4 %all-to-all-start = ((bf16[4,8,10890]{2,0,1:T(4,128)(2,1)}), bf16[4,8,10890]{2,0,1:T(4,128)(2,1)}, u32[]{:S(2)}, u32[]{:S(2)}) async-start(bf16[4,8,10890]{2,0,1:T(4,128)(2,1)} %copy.262), calls=%async_computation | async-start | bytes 1409024 | tf_op jit(solution)/shard_map/all_to_all | solution.py:40
  30.0 3.6 %copy-start.13 = (f32[641,8]{0,1:T(8,128)S(1)}, f32[641,8]{0,1:T(8,128)}, u32[]{:S(2)}) copy-start(f32[641,8]{0,1:T(8,128)} %param.12) | copy-start | bytes 61540
  33.9 14.5 %copy-start.5 = (f32[9,8,2,361,8]{3,2,1,0,4:T(2,128)S(1)}, f32[9,8,2,361,8]{3,2,1,0,4:T(2,128)}, u32[]{:S(2)}) copy-start(f32[9,8,2,361,8]{3,2,1,0,4:T(2,128)} %dot_general.26) | copy-start | bytes 4990468
  33.9 14.5 %copy-start.12 = (s32[4]{0:T(128)S(1)}, s32[4]{0:T(128)}, u32[]{:S(2)}) copy-start(s32[4]{0:T(128)} %param.10) | copy-start | bytes 52
  57.2 32.6 %copy-start.1 = (bf16[4,8,121,90]{3,2,1,0:T(8,128)(2,1)}, bf16[4,8,121,90]{3,2,1,0:T(8,128)(2,1)S(1)}, u32[]{:S(2)}) copy-start(bf16[4,8,121,90]{3,2,1,0:T(8,128)(2,1)S(1)} %reshape.469) | copy-start | bytes 2090884
  58.7 31.1 %collective-permute-start = (bf16[4,8,121,90]{2,1,3,0:T(8,128)(2,1)}, bf16[4,8,121,90]{2,1,3,0:T(8,128)(2,1)}, u32[]{:S(2)}, u32[]{:S(2)}) collective-permute-start(bf16[4,8,121,90]{2,1,3,0:T(8,128)(2,1)} %copy.264), channel_id=1, source_target_pairs={{0,8},{8,16},{16,24},{1,9},{9,17},{17,25},{2,10},{10,18},{18,26},{... | collective-permute-start | bytes 2090888 | tf_op jit(solution)/shard_map/ppermute | solution.py:22
  62.9 33.6 %collective-permute-start.1 = (bf16[4,8,121,90]{2,1,3,0:T(8,128)(2,1)}, bf16[4,8,121,90]{2,1,3,0:T(8,128)(2,1)}, u32[]{:S(2)}, u32[]{:S(2)}) collective-permute-start(bf16[4,8,121,90]{2,1,3,0:T(8,128)(2,1)} %copy.264), channel_id=1, source_target_pairs={{8,0},{16,8},{24,16},{9,1},{17,9},{25,17},{10,2},{18,10},{26,18},{... | collective-permute-start | bytes 2090888 | tf_op jit(solution)/shard_map/ppermute | solution.py:24
  96.5 26.3 %slice-start = ((s8[13565952]{0:T(1024)(128)(4,1)}), s8[983040]{0:T(1024)(128)(4,1)S(1)}, s32[]{:S(2)}) async-start(s8[13565952]{0:T(1024)(128)(4,1)} %bitcast.242), calls=%async_computation.2 | async-start | bytes 1966080
  99.0 3.1 %copy-start.2 = (bf16[4,8,121,90]{3,2,1,0:T(8,128)(2,1)S(1)}, bf16[4,8,121,90]{3,2,1,0:T(8,128)(2,1)}, u32[]{:S(2)}) copy-start(bf16[4,8,121,90]{3,2,1,0:T(8,128)(2,1)} %copy-done.1) | copy-start | bytes 2090884
  99.0 3.1 %copy-start.3 = (bf16[4,8,121,90]{3,2,1,0:T(8,128)(2,1)S(1)}, bf16[4,8,121,90]{3,2,1,0:T(8,128)(2,1)}, u32[]{:S(2)}) copy-start(bf16[4,8,121,90]{3,2,1,0:T(8,128)(2,1)} %copy.270) | copy-start | bytes 2090884
  99.0 3.1 %copy-start.4 = (bf16[4,8,121,90]{3,2,1,0:T(8,128)(2,1)S(1)}, bf16[4,8,121,90]{3,2,1,0:T(8,128)(2,1)}, u32[]{:S(2)}) copy-start(bf16[4,8,121,90]{3,2,1,0:T(8,128)(2,1)} %copy.271) | copy-start | bytes 2090884
  102.1 2.0 %copy-start.10 = (f32[8,90,1,361]{3,1,0,2:T(8,128)S(1)}, f32[8,90,1,361]{3,1,0,2:T(8,128)}, u32[]{:S(2)}) copy-start(f32[8,90,1,361]{3,1,0,2:T(8,128)} %get-tuple-element.15) | copy-start | bytes 3119044
  102.1 2.0 %copy-start.11 = (f32[8,90,1,361]{3,1,0,2:T(8,128)S(1)}, f32[8,90,1,361]{3,1,0,2:T(8,128)}, u32[]{:S(2)}) copy-start(f32[8,90,1,361]{3,1,0,2:T(8,128)} %get-tuple-element.16) | copy-start | bytes 3119044
  102.1 20.7 %slice-start.1 = ((s8[13565952]{0:T(1024)(128)(4,1)}), s8[4194304]{0:T(1024)(128)(4,1)S(1)}, s32[]{:S(2)}) async-start(s8[13565952]{0:T(1024)(128)(4,1)} %bitcast.242), calls=%async_computation.3 | async-start | bytes 8388608
  104.1 18.8 %slice-start.2 = ((s8[13565952]{0:T(1024)(128)(4,1)}), s8[4194304]{0:T(1024)(128)(4,1)S(1)}, s32[]{:S(2)}) async-start(s8[13565952]{0:T(1024)(128)(4,1)} %bitcast.242), calls=%async_computation.4 | async-start | bytes 8388608
  104.1 18.8 %slice-start.3 = ((s8[13565952]{0:T(1024)(128)(4,1)}), s8[4194304]{0:T(1024)(128)(4,1)S(1)}, s32[]{:S(2)}) async-start(s8[13565952]{0:T(1024)(128)(4,1)} %bitcast.242), calls=%async_computation.5 | async-start | bytes 8388608
  124.7 2.3 %copy-start.6 = (f32[1,361,8,90]{1,3,0,2:T(8,128)S(1)}, f32[1,361,8,90]{1,3,0,2:T(8,128)}, u32[]{:S(2)}) copy-start(f32[1,361,8,90]{1,3,0,2:T(8,128)} %get-tuple-element.11) | copy-start | bytes 3119044
  124.7 2.3 %copy-start.7 = (f32[1,361,8,90]{1,3,0,2:T(8,128)S(1)}, f32[1,361,8,90]{1,3,0,2:T(8,128)}, u32[]{:S(2)}) copy-start(f32[1,361,8,90]{1,3,0,2:T(8,128)} %get-tuple-element.12) | copy-start | bytes 3119044
  127.0 4.1 %copy-start.9 = (bf16[4,8,121,90]{2,1,3,0:T(8,128)(2,1)S(1)}, bf16[4,8,121,90]{2,1,3,0:T(8,128)(2,1)}, u32[]{:S(2)}) copy-start(bf16[4,8,121,90]{2,1,3,0:T(8,128)(2,1)} %copy.264) | copy-start | bytes 2090884
  138.3 23.9 %all-to-all-start.1 = ((bf16[4,8,10890]{2,0,1:T(4,128)(2,1)}), bf16[4,8,10890]{2,0,1:T(4,128)(2,1)S(1)}, u32[]{:S(2)}, u32[]{:S(2)}) async-start(bf16[4,8,10890]{2,0,1:T(4,128)(2,1)} %reshape.543), calls=%async_computation.1 | async-start | bytes 1409024 | tf_op jit(solution)/shard_map/all_to_all | solution.py:117
  171.6 4.4 %copy-start.14 = (f32[641]{0:T(1024)S(1)}, f32[641]{0:T(1024)}, u32[]{:S(2)}) copy-start(f32[641]{0:T(1024)} %param.13) | copy-start | bytes 7696
  173.3 2.7 %copy-start.8 = (f32[360,641]{0,1:T(8,128)S(1)}, f32[360,641]{0,1:T(8,128)}, u32[]{:S(2)}) copy-start(f32[360,641]{0,1:T(8,128)} %reshape.544) | copy-start | bytes 2769124
where the time goes:
time: 190 us; the launch traced here: 187 us
  matrix products  58.2 us (31%)
  local copies, waits for them, and re-layouts  53.2 us (28%)
  other arithmetic  38.4 us (20%)
  waiting for transfers between devices  18.3 us (10%)
  starting transfers between devices  17.3 us (9%)
    dot_general x1, matrix products, per_device(): jnp.einsum('gb,rdbpk->rdgpk', slot_coef, row_basis, precision=lax.Precisi...  24.8 us
    dot_general x1, matrix products, forward(): jnp.einsum('rngc,ncpk->rgpk', normed, forward_table, precision=lax.Precis...  18.7 us
    all_to_all x1, waiting for transfers between devices, per_device(): lax.all_to_all(outgoing, 'lon', split_axis=1, concat_axis=1, tiled=True)  14 us
    dot_general x1, matrix products, per_device(): result = inputs + jnp.dot(hidden, w_out, preferred_element_type=jnp.float32)  8.1 us
    gather x1, local copies, waits for them, and re-layouts, to_groups(): jnp.take(block, send_index, axis=2)  7.52 us
    mul x1, other arithmetic, per_device(): cosine * inv_weight  7.27 us
    cos x1, other arithmetic, per_device(): cosine = jnp.cos(angle)  7.21 us
    all_to_all x1, starting transfers between devices, to_groups(): lax.all_to_all(packed, 'lon', split_axis=1, concat_axis=1, tiled=True)  6.93 us
  transfers between devices with their start and end apart: 4, of which 2 were waited for; matrix products, arithmetic and copies ran while one was open for 31% of the time, Pallas kernels for 0%

commit v1 on v0

v1 whole, which is shorter than its diff:
```python
import functools
import math

import jax
import jax.numpy as jnp
import numpy as np
from jax import lax
from jax.experimental import pallas as pl
from jax.experimental.pallas import tpu as pltpu
from jax.sharding import PartitionSpec as P

HALO = 4
TAPS = 2 * HALO + 1
EPSILON = 1e-05
AXES = ("lat", "lon")
VMEM = pl.BlockSpec(memory_space=pltpu.VMEM)
SMEM = pl.BlockSpec(memory_space=pltpu.SMEM)
PARAMS = pltpu.CompilerParams(vmem_limit_bytes=60 * 1024 * 1024)


def round_up(value, step):
    return -(-value // step) * step


def dft_tables(lon_count, pieces, width, bins):
    cols = lon_count // pieces
    freq = lon_count // 2 + 1
    phase = np.arange(lon_count)[:, None] * np.arange(freq)[None, :] % lon_count
    angle = phase * (2.0 * math.pi / lon_count)
    cosine = np.cos(angle)
    sine = np.where(2 * phase % lon_count == 0, 0.0, np.sin(angle))
    index = np.arange(freq)
    weight = np.where((index == 0) | (2 * index == lon_count), 1.0, 2.0) / lon_count
    forward = np.zeros((pieces, width, 2, bins), np.float64)
    inverse = np.zeros((pieces, width, 2, bins), np.float64)
    forward[:, :cols, 0, :freq] = cosine.reshape(pieces, cols, freq)
    forward[:, :cols, 1, :freq] = -sine.reshape(pieces, cols, freq)
    inverse[:, :cols, 0, :freq] = (cosine * weight).reshape(pieces, cols, freq)
    inverse[:, :cols, 1, :freq] = (-sine * weight).reshape(pieces, cols, freq)
    forward = forward.reshape(pieces * width, 2 * bins).astype(jnp.bfloat16)
    inverse = inverse.reshape(pieces * width, 2 * bins).T.astype(jnp.bfloat16)
    total = forward.astype(np.float64).sum(axis=0, keepdims=True).astype(np.float32)
    return forward, inverse, total


def kernel_body(coef_ref, basis_ref, out_ref):
    coef = coef_ref[...]

    def step(n, carry):
        basis = basis_ref[n]
        high = basis.astype(jnp.bfloat16)
        low = (basis - high.astype(jnp.float32)).astype(jnp.bfloat16)
        both = jnp.concatenate([high, high, low], axis=0)
        out_ref[n] = jnp.dot(coef, both, preferred_element_type=jnp.float32)
        return carry

    lax.fori_loop(0, basis_ref.shape[0], step, 0, unroll=4)


def corr_body(
    pieces, rows, cols, width, bins,
    band_ref, block_ref, forward_ref, inverse_ref, total_ref, mean_ref, scale_ref, kern_ref,
    out_ref, wide_ref, spec_ref, prod_ref, corr_ref,
):
    chan = block_ref.shape[1]
    bands = block_ref.shape[0] // pieces
    lat = bands * rows
    wide_ref[...] = jnp.zeros_like(wide_ref)
    for band in range(bands):
        for piece in range(pieces):
            cells = block_ref[band * pieces + piece].astype(jnp.float32)
            for row in range(rows):
                at = (band * rows + row) * chan
                wide_ref[at : at + chan, piece * width : piece * width + cols] = cells[
                    :, row * cols : (row + 1) * cols
                ]
    raw = jnp.dot(
        wide_ref[...].astype(jnp.bfloat16), forward_ref[...], preferred_element_type=jnp.float32
    )
    spec_ref[...] = (raw - mean_ref[...] * total_ref[...]) * scale_ref[...]
    for row in range(lat):
        band = band_ref[row]
        real = jnp.zeros((chan, bins), jnp.float32)
        imag = jnp.zeros((chan, bins), jnp.float32)
        for tap in range(TAPS):
            source = row + tap - HALO
            if source < 0 or source >= lat:
                continue
            spec_real = spec_ref[source * chan : (source + 1) * chan, :bins]
            spec_imag = spec_ref[source * chan : (source + 1) * chan, bins:]
            kern_real = kern_ref[band * TAPS + tap, :chan]
            kern_imag = kern_ref[band * TAPS + tap, chan:]
            real = real + kern_real * spec_real - kern_imag * spec_imag
            imag = imag + kern_real * spec_imag + kern_imag * spec_real
        prod_ref[row * chan : (row + 1) * chan, :bins] = real
        prod_ref[row * chan : (row + 1) * chan, bins:] = imag
    corr_ref[...] = jnp.dot(
        prod_ref[...].astype(jnp.bfloat16), inverse_ref[...], preferred_element_type=jnp.float32
    )
    for band in range(bands):
        for piece in range(pieces):
            parts = []
            for row in range(rows):
                at = (band * rows + row) * chan
                parts.append(
                    corr_ref[at : at + chan, piece * width : piece * width + cols]
                )
            cells = block_ref[band * pieces + piece].astype(jnp.float32)
            out_ref[band * pieces + piece] = (
                cells + jnp.concatenate(parts, axis=1)
            ).astype(jnp.bfloat16)


def per_device(fields, group_size, band_of_row, basis_spectra, basis_coef, mlp_gain, w_in, w_out):
    row_count, col_count, chan_count = fields.shape
    pieces = lax.axis_size("lon")
    bands = lax.axis_size("lat")
    devices = pieces * bands
    lon_count = col_count * pieces
    lat_count = row_count * bands
    freq_count = lon_count // 2 + 1
    groups = group_size.shape[0]
    pixels = row_count * col_count
    chan = round_up(-(-chan_count // devices), 8)
    held = devices * chan
    width = round_up(col_count, 128)
    bins = round_up(freq_count, 128)
    band_count, _, basis_count = basis_spectra.shape[:3]
    me = lax.axis_index(AXES)

    turned = jnp.transpose(fields, (2, 0, 1)).reshape(chan_count, pixels)
    turned = jnp.pad(turned, ((0, held - chan_count), (0, 0))).reshape(devices, chan, pixels)
    arrived = lax.all_to_all(turned, AXES, split_axis=0, concat_axis=0, tiled=True)

    starts = jnp.cumsum(group_size) - group_size
    channel = jnp.arange(held, dtype=jnp.int32)
    within = (channel[:, None] >= starts[None, :]) & (
        channel[:, None] < (starts + group_size)[None, :]
    )
    member = within.astype(jnp.float32)
    local = member[:chan_count]
    values = fields.astype(jnp.float32)
    amount = group_size.astype(jnp.float32) * col_count
    centre = (
        jnp.dot(jnp.sum(values, axis=1), local, precision=lax.Precision.HIGHEST) / amount
    )
    middle = jnp.dot(centre, local.T, precision=lax.Precision.HIGHEST)
    offset = values - middle[:, None, :]
    squares = jnp.dot(jnp.sum(offset * offset, axis=1), local, precision=lax.Precision.HIGHEST)
    report = jnp.concatenate(
        [centre.reshape(-1), squares.reshape(-1), band_of_row.astype(jnp.float32)]
    )
    reports = lax.all_gather(report, AXES, axis=0, tiled=False)
    count = row_count * groups
    centres = reports[:, :count].reshape(bands, pieces, row_count, groups)
    spreads = reports[:, count : 2 * count].reshape(bands, pieces, row_count, groups)
    band_rows = reports[:, 2 * count :].reshape(bands, pieces, row_count)[:, 0].reshape(-1)
    band_rows = band_rows.astype(jnp.int32)
    mean = jnp.mean(centres, axis=1)
    total = jnp.sum(spreads + amount * (centres - mean[:, None]) ** 2, axis=1)
    scale = lax.rsqrt(total / (amount * pieces) + EPSILON)
    mine = lax.dynamic_slice_in_dim(member, me * chan, chan, axis=0)
    pick = functools.partial(jnp.einsum, "irg,cg->irc", precision=lax.Precision.HIGHEST)
    mean = pick(mean, mine).reshape(lat_count * chan, 1)
    scale = pick(scale, mine).reshape(lat_count * chan, 1)

    coef = jnp.pad(basis_coef, ((0, held - chan_count), (0, 0)))
    coef = lax.dynamic_slice_in_dim(coef, me * chan, chan, axis=0)
    coef = jnp.einsum("cb,pq->pcbq", coef, jnp.eye(2, dtype=jnp.float32))
    coef = coef.reshape(2 * chan, 2 * basis_count)
    high = coef.astype(jnp.bfloat16)
    low = (coef - high.astype(jnp.float32)).astype(jnp.bfloat16)
    coef = jnp.concatenate([high, low, high], axis=1)
    basis = basis_spectra.reshape(band_count * TAPS, 2 * basis_count, freq_count)
    basis = jnp.pad(basis, ((0, 0), (0, 0), (0, bins - freq_count)))
    kern = pl.pallas_call(
        kernel_body,
        out_shape=jax.ShapeDtypeStruct((band_count * TAPS, 2 * chan, bins), jnp.float32),
        in_specs=[VMEM] * 2,
        out_specs=VMEM,
        compiler_params=PARAMS,
        cost_estimate=pl.CostEstimate(
            flops=2 * 72 * 48 * 48 * 384, bytes_accessed=10_000_000, transcendentals=0
        ),
    )(coef, basis)

    forward, inverse, sums = dft_tables(lon_count, pieces, width, bins)
    mixed = pl.pallas_call(
        functools.partial(corr_body, pieces, row_count, col_count, width, bins),
        out_shape=jax.ShapeDtypeStruct((devices, chan, pixels), jnp.bfloat16),
        in_specs=[SMEM] + [VMEM] * 7,
        out_specs=VMEM,
        scratch_shapes=[
            pltpu.VMEM((lat_count * chan, pieces * width), jnp.float32),
            pltpu.VMEM((lat_count * chan, 2 * bins), jnp.float32),
            pltpu.VMEM((lat_count * chan, 2 * bins), jnp.float32),
            pltpu.VMEM((lat_count * chan, pieces * width), jnp.float32),
        ],
        compiler_params=PARAMS,
    )(band_rows, arrived, forward, inverse, sums, mean, scale, kern)
    returned = lax.all_to_all(mixed, AXES, split_axis=0, concat_axis=0, tiled=True)
    inputs = returned.reshape(held, pixels)[:chan_count].T.astype(jnp.float32)
    centre = jnp.mean(inputs, axis=-1, keepdims=True)
    spread = jnp.mean((inputs - centre) ** 2, axis=-1, keepdims=True)
    normalised = ((inputs - centre) * lax.rsqrt(spread + EPSILON) * mlp_gain).astype(jnp.bfloat16)
    hidden = jax.nn.gelu(
        jnp.dot(normalised, w_in, preferred_element_type=jnp.float32), approximate=False
    ).astype(jnp.bfloat16)
    result = inputs + jnp.dot(hidden, w_out, preferred_element_type=jnp.float32)
    return result.astype(jnp.bfloat16).reshape(row_count, col_count, chan_count)


def solution(mesh):
    placed = (P("lat", "lon", None), P(), P("lat"), P(), P(), P(), P(), P())
    return jax.shard_map(
        per_device, mesh=mesh, in_specs=placed, out_specs=P("lat", "lon", None), check_vma=False
    )
```

time: 190 us -> 113 us (0.59); the launches traced: 187 us -> 113 us
  blocking collectives: 0 us -> 62.9 us
  matrix products: 58.2 us -> 8.62 us
  local copies, waits for them, and re-layouts: 53.2 us -> 16.1 us
  other arithmetic: 38.4 us -> 2.32 us
  waiting for transfers between devices: 18.3 us -> 0.01 us
  Pallas kernels: 0 us -> 15.4 us
  starting transfers between devices: 17.3 us -> 7.33 us
    dot_general x5, matrix products: 50.1 us -> 0.82 us  [the longest x1 0.21 us: per_device(): mean = pick(mean, mine).reshape(lat_count * chan, 1)]
    unnamed x0 -> x1, blocking collectives: none -> 40.9 us
    all_to_all x0 -> x1, blocking collectives: none -> 22 us  [per_device(): lax.all_to_all(mixed, AXES, split_axis=0, concat_axis=0, tiled=True)]
    reshape x9 -> x10, local copies, waits for them, and re-layouts: 22 us -> 5.56 us  [the longest x1 3.38 us: per_device(): basis_spectra.reshape(band_count * TAPS, 2 * basis_count, freq_count)]
    pallas_call x0 -> x2, Pallas kernels: none -> 15.4 us  [the longest x1 8.22 us: per_device(): pl.pallas_call(functools.partial(corr_body, pieces, row_count, col_count,...]
    all_to_all x2 -> x1, waiting for transfers between devices: 14 us -> 0.01 us  [per_device(): lax.all_to_all(turned, AXES, split_axis=0, concat_axis=0, tiled=True)]
    gather x3 -> x0, local copies, waits for them, and re-layouts: 11.1 us -> none  [the longest x1 7.52 us: to_groups(): jnp.take(block, send_index, axis=2)]
    mul x2 -> x1, other arithmetic: 7.28 us -> 0.01 us  [per_device(): scale = lax.rsqrt(total / (amount * pieces) + EPSILON)]
  transfers between devices with their start and end apart: 4 -> 1, of which waited for: 2 -> 0; matrix products, arithmetic and copies ran while one was open for 31% -> 11% of each run, Pallas kernels for 0% -> 6%
where the time goes in v1:
time: 113 us
  blocking collectives  62.9 us (56%)
  local copies, waits for them, and re-layouts  16.1 us (14%)
  Pallas kernels  15.4 us (14%)
  matrix products  8.62 us (8%)
  starting transfers between devices  7.33 us (6%)
  other arithmetic  2.32 us (2%)
    unnamed x1, blocking collectives  40.9 us
    all_to_all x1, blocking collectives, per_device(): lax.all_to_all(mixed, AXES, split_axis=0, concat_axis=0, tiled=True)  22 us
    pallas_call x1, Pallas kernels, per_device(): pl.pallas_call(functools.partial(corr_body, pieces, row_count, col_count,...  8.22 us
    dot_general x1, matrix products, per_device(): result = inputs + jnp.dot(hidden, w_out, preferred_element_type=jnp.float32)  7.8 us
    all_to_all x1, starting transfers between devices, per_device(): lax.all_to_all(turned, AXES, split_axis=0, concat_axis=0, tiled=True)  7.33 us
    pallas_call x1, Pallas kernels, per_device(): pl.pallas_call(kernel_body, out_shape=jax.ShapeDtypeStruct((band_count *...  7.18 us
    unnamed x17, local copies, waits for them, and re-layouts  3.5 us
    reshape x1, local copies, waits for them, and re-layouts, per_device(): basis_spectra.reshape(band_count * TAPS, 2 * basis_count, freq_count)  3.38 us
  transfers between devices with their start and end apart: 1, of which 0 were waited for; matrix products, arithmetic and copies ran while one was open for 11% of the time, Pallas kernels for 6%

profile of v1, /device:TPU:0, one launch (start us, length us, event | category | flops | bytes accessed | tf_op | source)
XLA Modules:
  0.0 112.9 jit_solution(14592259430756190561)
XLA Ops:
  0.0 0.0 copy-start
  0.0 1.9 %copy.44 = bf16[641,4,90]{2,1,0:T(4,128)(2,1)S(1)} copy(bf16[641,4,90]{0,1,2:T(4,128)(2,1)} %bitcast.48) | data formatting | bytes 923040
  2.0 0.0 copy-start.1
  2.0 0.0 copy-start.5
  2.0 0.7 reshape.106
  2.6 0.0 copy-start.6
  2.7 0.0 copy-start.3
  2.7 0.9 pad.12.clone
  3.5 7.3 %all-to-all-start = ((bf16[32,24,360]{2,1,0:T(8,128)(2,1)}), bf16[32,24,360]{2,1,0:T(8,128)(2,1)S(1)}, u32[]{:S(2)}, u32[]{:S(2)}) async-start(bf16[32,24,360]{2,1,0:T(8,128)(2,1)} %bitcast.52), calls=%async_computation | async-start | bytes 1179648 | tf_op jit(solution)/shard_map/all_to_all | solution.py:133
  10.9 0.3 convert_reduce_fusion
  11.2 0.2 reduce-window.8
  11.4 0.1 fusion.63
  11.4 0.1 convolution_divide_fusion
  11.5 0.2 fusion.66
  11.7 0.1 reshape.86
  11.8 0.4 fusion.15
  12.2 0.1 fusion.64
  12.3 0.1 reshape.87
  12.4 0.2 maximum_dynamic-update-slice_fusion
  12.6 40.9 %all-reduce.3 = f32[2176]{0:T(1024)S(1)} all-reduce(f32[2176]{0:T(1024)S(1)} %maximum_dynamic-update-slice_fusion), channel_id=2, replica_groups=mesh['lat'=4,'lon'=8] {'lat','lon'}, use_global_device_ids=true, to_apply=%add.3 | all-reduce | flops 2176 | bytes 17408
  53.5 0.1 reshape.99
  53.6 0.1 fusion.113
  53.7 0.1 reshape.91
  53.9 0.1 reshape.93
  54.0 0.1 pad_dynamic-slice_fusion
  54.1 0.1 multiply_bitcast_fusion
  54.2 0.1 reshape.95
  54.3 0.1 copy.31
  54.3 0.2 fusion.69
  54.6 0.8 reshape.104.scale_ref
  55.4 0.1 copy.32
  55.4 3.4 %reshape.96 = f32[72,16,361]{2,1,0:T(8,128)} reshape(f32[8,9,8,2,361]{4,3,2,1,0:T(2,128)} %param.14) | data formatting | bytes 3326976 | tf_op jit(solution)/shard_map/reshape | solution.py:174
  58.8 2.8 %pad.14.basis_ref = f32[72,16,384]{2,1,0:T(8,128)} pad(f32[72,16,361]{2,1,0:T(8,128)} %reshape.96, f32[]{:T(128)} %constant.45.clone.1), padding=0_0x0_0x0_23 | pad | bytes 3432964 | tf_op jit(solution)/shard_map/jit(_pad)/pad | solution.py:175
  61.7 0.2 fusion.76
  61.9 0.8 reshape.103.mean_ref
  62.7 0.1 slice_bitcast_fusion
  62.8 0.6 convert_element_type.50.band_ref
  63.4 0.7 pad_maximum_fusion.coef_ref
  64.1 7.2 %shard_map.109.kern_ref = f32[72,48,384]{2,1,0:T(8,128)} custom-call(bf16[48,48]{1,0:T(8,128)(2,1)} %pad_maximum_fusion.coef_ref, f32[72,16,384]{2,1,0:T(8,128)} %pad.14.basis_ref), custom_call_target="tpu_custom_call" | custom-call | flops 127401984 | bytes 10000000 | tf_op jit(solution)/shard_map/pallas_call | solution.py:176
  71.3 0.0 all-to-all-done.block_ref
  71.3 0.8 copy-done.2
  72.1 8.2 %shard_map.110 = bf16[32,24,360]{2,1,0:T(8,128)(2,1)} custom-call(s32[16]{0:T(128)} %convert_element_type.50.band_ref, bf16[32,24,360]{2,1,0:T(8,128)(2,1)} %copy-done.2, bf16[1024,768]{1,0:T(8,128)(2,1)} %constant.104.clone.forward_ref, bf16[768,1024]{1,0:T(8,128)(2,1)} %constant.105.clone.inverse_ref, f32[1,768]{1,0:T(1,128)} %constant.106.clone.total_ref, ...), custom_call_target="tpu_custom_call" | custom-call | tf_op jit(solution)/shard_map/pallas_call | solution.py:188
  80.3 22.0 %all_to_all.10 = bf16[32,24,360]{2,1,0:T(8,128)(2,1)S(1)} all-to-all(bf16[32,24,360]{2,1,0:T(8,128)(2,1)} %shard_map.110), channel_id=1, replica_groups=mesh['lat'=4,'lon'=8] {'lat','lon'}, dimensions={0} | all-to-all | bytes 1105920 | tf_op jit(solution)/shard_map/all_to_all | solution.py:201
  102.3 0.1 convert_reduce_fusion.1
  102.5 0.2 fusion.16
  102.7 7.8 %fusion.10 = bf16[360,641]{0,1:T(8,128)(2,1)S(1)} fusion(bf16[1282,641]{0,1:T(8,128)(2,1)S(1)} %copy-done, bf16[641,1282]{1,0:T(8,128)(2,1)} %param.17, f32[641]{0:T(1024)S(1)} %copy-done.4, f32[360]{0:T(512)S(1)} %add_rsqrt_fusion, f32[360]{0:T(512)S(1)} %broadcast_multiply_fusion.1, bf16[768,360]{1,0:T(8,128)(2,1)S(1)} %bitcast.51), kind=kOutput, calls=%fused_computation.22 | convolution fusion | flops 1215181056 | bytes 4933332 | tf_op jit(solution)/shard_map/dot_general | solution.py:209
  110.5 0.8 reshape.105
  111.3 1.6 %copy.37 = bf16[4,90,641]{2,0,1:T(4,128)(2,1)} copy(bf16[4,90,641]{1,0,2:T(4,128)(2,1)S(1)} %reshape.105) | data formatting | bytes 923040 | tf_op jit(solution)/shard_map/reshape | solution.py:210
  (22 shorter events, 0.2 us)
Async XLA Ops:
  0.0 102.7 %copy-start = (bf16[1282,641]{0,1:T(8,128)(2,1)S(1)}, bf16[1282,641]{0,1:T(8,128)(2,1)}, u32[]{:S(2)}) copy-start(bf16[1282,641]{0,1:T(8,128)(2,1)} %param.18) | copy-start | bytes 4930576
  2.0 8.9 %copy-start.1 = (bf16[4,90,641]{2,0,1:T(4,128)(2,1)S(1)}, bf16[4,90,641]{2,0,1:T(4,128)(2,1)}, u32[]{:S(2)}) copy-start(bf16[4,90,641]{2,0,1:T(4,128)(2,1)} %param.11) | copy-start | bytes 1384564
  2.0 9.2 %copy-start.5 = (s32[8]{0:T(128)S(1)}, s32[8]{0:T(128)}, u32[]{:S(2)}) copy-start(s32[8]{0:T(128)} %param.12) | copy-start | bytes 100
  2.6 9.8 %copy-start.6 = (s32[4]{0:T(128)S(1)}, s32[4]{0:T(128)}, u32[]{:S(2)}) copy-start(s32[4]{0:T(128)} %param.13) | copy-start | bytes 52
  2.7 51.3 %copy-start.3 = (f32[641,8]{0,1:T(8,128)S(1)}, f32[641,8]{0,1:T(8,128)}, u32[]{:S(2)}) copy-start(f32[641,8]{0,1:T(8,128)} %param.15) | copy-start | bytes 61540
  3.5 67.7 %all-to-all-start = ((bf16[32,24,360]{2,1,0:T(8,128)(2,1)}), bf16[32,24,360]{2,1,0:T(8,128)(2,1)S(1)}, u32[]{:S(2)}, u32[]{:S(2)}) async-start(bf16[32,24,360]{2,1,0:T(8,128)(2,1)} %bitcast.52), calls=%async_computation | async-start | bytes 1179648 | tf_op jit(solution)/shard_map/all_to_all | solution.py:133
  71.3 0.8 copy-start.2
  80.3 22.3 %copy-start.4 = (f32[641]{0:T(1024)S(1)}, f32[641]{0:T(1024)}, u32[]{:S(2)}) copy-start(f32[641]{0:T(1024)} %param.16) | copy-start | bytes 7696

commit v2 on v1

--- a/solution.py
+++ b/solution.py
@@ -12,9 +12,10 @@
 HALO = 4
 TAPS = 2 * HALO + 1
 EPSILON = 1e-05
-AXES = ("lat", "lon")
 VMEM = pl.BlockSpec(memory_space=pltpu.VMEM)
 SMEM = pl.BlockSpec(memory_space=pltpu.SMEM)
+MESH = pl.DeviceIdType.MESH
+DMA = pltpu.SemaphoreType.DMA
 PARAMS = pltpu.CompilerParams(vmem_limit_bytes=60 * 1024 * 1024)
 
 
@@ -31,35 +32,151 @@
     sine = np.where(2 * phase % lon_count == 0, 0.0, np.sin(angle))
     index = np.arange(freq)
     weight = np.where((index == 0) | (2 * index == lon_count), 1.0, 2.0) / lon_count
-    forward = np.zeros((pieces, width, 2, bins), np.float64)
-    inverse = np.zeros((pieces, width, 2, bins), np.float64)
-    forward[:, :cols, 0, :freq] = cosine.reshape(pieces, cols, freq)
-    forward[:, :cols, 1, :freq] = -sine.reshape(pieces, cols, freq)
-    inverse[:, :cols, 0, :freq] = (cosine * weight).reshape(pieces, cols, freq)
-    inverse[:, :cols, 1, :freq] = (-sine * weight).reshape(pieces, cols, freq)
-    forward = forward.reshape(pieces * width, 2 * bins).astype(jnp.bfloat16)
-    inverse = inverse.reshape(pieces * width, 2 * bins).T.astype(jnp.bfloat16)
-    total = forward.astype(np.float64).sum(axis=0, keepdims=True).astype(np.float32)
-    return forward, inverse, total
-
-
-def kernel_body(coef_ref, basis_ref, out_ref):
+    table = np.zeros((pieces, width, 2, bins), np.float64)
+    table[:, :cols, 0, :freq] = cosine.reshape(pieces, cols, freq)
+    table[:, :cols, 1, :freq] = -sine.reshape(pieces, cols, freq)
+    table = table.reshape(pieces * width, 2 * bins).astype(jnp.bfloat16)
+    total = table.astype(np.float64).sum(axis=0, keepdims=True).astype(np.float32)
+    scaled = np.zeros((2, bins), np.float32)
+    scaled[:, :freq] = weight
+    return table, total, scaled.reshape(1, 2 * bins)
+
+
+def place(index):
+    pieces = lax.axis_size("lon")
+    return (lax.div(index, pieces), lax.rem(index, pieces))
+
+
+def greet(devices, me):
+    barrier = pltpu.get_barrier_semaphore()
+
+    def signal(step, carry):
+        pl.semaphore_signal(
+            barrier, inc=1, device_id=place(lax.rem(me + step, devices)), device_id_type=MESH
+        )
+        return carry
+
+    lax.fori_loop(1, devices, signal, 0)
+    pl.semaphore_wait(barrier, devices - 1)
+
+
+def own_index():
+    return lax.axis_index("lat") * lax.axis_size("lon") + lax.axis_index("lon")
+
+
+def drain(blocks, amount, semaphore):
+    part = blocks.at[pl.ds(0, amount)]
+    pltpu.make_async_copy(part, part, semaphore).wait()
+
+
+def scatter_body(
+    devices, active, freq,
+    block_ref, report_ref, coef_ref, basis_ref,
+    arrived_ref, reports_ref, kern_ref,
+    send_sem, recv_sem, report_send_sem, report_recv_sem, local_sem,
+):
+    me = own_index()
+    greet(devices, me)
+
+    def send(step, carry):
+        target = lax.rem(me + step, devices)
+        pltpu.make_async_remote_copy(
+            src_ref=report_ref,
+            dst_ref=reports_ref.at[me],
+            send_sem=report_send_sem,
+            recv_sem=report_recv_sem,
+            device_id=place(target),
+            device_id_type=MESH,
+        ).start()
+
+        @pl.when(target < active)
+        def _():
+            pltpu.make_async_remote_copy(
+                src_ref=block_ref.at[target],
+                dst_ref=arrived_ref.at[me],
+                send_sem=send_sem,
+                recv_sem=recv_sem,
+                device_id=place(target),
+                device_id_type=MESH,
+            ).start()
+
+        return carry
+
+    lax.fori_loop(1, devices, send, 0)
+    reports_ref[me] = report_ref[...]
+    own = pltpu.make_async_copy(
+        block_ref.at[lax.rem(me, active)], arrived_ref.at[me], local_sem
+    )
+    own.start()
+
+    chan, bins = kern_ref.shape[1] // 2, kern_ref.shape[2]
     coef = coef_ref[...]
-
-    def step(n, carry):
-        basis = basis_ref[n]
-        high = basis.astype(jnp.bfloat16)
-        low = (basis - high.astype(jnp.float32)).astype(jnp.bfloat16)
-        both = jnp.concatenate([high, high, low], axis=0)
-        out_ref[n] = jnp.dot(coef, both, preferred_element_type=jnp.float32)
+    blank = jnp.zeros((basis_ref.shape[1], bins - freq), jnp.float32)
+
+    def generate(n, carry):
+        for part in range(2):
+            basis = jnp.concatenate([basis_ref[n, :, part, :], blank], axis=1)
+            high = basis.astype(jnp.bfloat16).astype(jnp.float32)
+            both = jnp.concatenate([high, high, basis - high], axis=0).astype(jnp.bfloat16)
+            kern_ref[n, part * chan : (part + 1) * chan] = jnp.dot(
+                coef, both, preferred_element_type=jnp.float32
+            )
         return carry
 
-    lax.fori_loop(0, basis_ref.shape[0], step, 0, unroll=4)
+    lax.fori_loop(0, basis_ref.shape[0], generate, 0)
+    own.wait()
+    drain(reports_ref, devices - 1, report_send_sem)
+    drain(reports_ref, devices - 1, report_recv_sem)
+
+    @pl.when(me < active)
+    def _():
+        drain(block_ref, active - 1, send_sem)
+        drain(arrived_ref, devices - 1, recv_sem)
+
+    @pl.when(me >= active)
+    def _():
+        drain(block_ref, active, send_sem)
+
+        def clear(n, carry):
+            arrived_ref[n] = jnp.zeros(arrived_ref.shape[1:], arrived_ref.dtype)
+            return carry
+
+        lax.fori_loop(0, devices, clear, 0)
+
+
+def gather_body(devices, active, mixed_ref, returned_ref, send_sem, recv_sem, local_sem):
+    me = own_index()
+    greet(devices, me)
+
+    @pl.when(me < active)
+    def _():
+        def send(step, carry):
+            target = lax.rem(me + step, devices)
+            pltpu.make_async_remote_copy(
+                src_ref=mixed_ref.at[target],
+                dst_ref=returned_ref.at[me],
+                send_sem=send_sem,
+                recv_sem=recv_sem,
+                device_id=place(target),
+                device_id_type=MESH,
+            ).start()
+            return carry
+
+        lax.fori_loop(1, devices, send, 0)
+        own = pltpu.make_async_copy(mixed_ref.at[me], returned_ref.at[me], local_sem)
+        own.start()
+        own.wait()
+        drain(mixed_ref, devices - 1, send_sem)
+        drain(returned_ref, active - 1, recv_sem)
+
+    @pl.when(me >= active)
+    def _():
+        drain(returned_ref, active, recv_sem)
 
 
 def corr_body(
     pieces, rows, cols, width, bins,
-    band_ref, block_ref, forward_ref, inverse_ref, total_ref, mean_ref, scale_ref, kern_ref,
+    band_ref, block_ref, table_ref, total_ref, weight_ref, mean_ref, scale_ref, kern_ref,
     out_ref, wide_ref, spec_ref, prod_ref, corr_ref,
 ):
     chan = block_ref.shape[1]
@@ -75,7 +192,7 @@
                     :, row * cols : (row + 1) * cols
                 ]
     raw = jnp.dot(
-        wide_ref[...].astype(jnp.bfloat16), forward_ref[...], preferred_element_type=jnp.float32
+        wide_ref[...].astype(jnp.bfloat16), table_ref[...], preferred_element_type=jnp.float32
     )
     spec_ref[...] = (raw - mean_ref[...] * total_ref[...]) * scale_ref[...]
     for row in range(lat):
@@ -94,8 +211,11 @@
             imag = imag + kern_real * spec_imag + kern_imag * spec_real
         prod_ref[row * chan : (row + 1) * chan, :bins] = real
         prod_ref[row * chan : (row + 1) * chan, bins:] = imag
-    corr_ref[...] = jnp.dot(
-        prod_ref[...].astype(jnp.bfloat16), inverse_ref[...], preferred_element_type=jnp.float32
+    corr_ref[...] = lax.dot_general(
+        (prod_ref[...] * weight_ref[...]).astype(jnp.bfloat16),
+        table_ref[...],
+        (((1,), (1,)), ((), ())),
+        preferred_element_type=jnp.float32,
     )
     for band in range(bands):
         for piece in range(pieces):
@@ -123,14 +243,15 @@
     pixels = row_count * col_count
     chan = round_up(-(-chan_count // devices), 8)
     held = devices * chan
+    active = -(-chan_count // chan)
     width = round_up(col_count, 128)
     bins = round_up(freq_count, 128)
     band_count, _, basis_count = basis_spectra.shape[:3]
-    me = lax.axis_index(AXES)
+    me = own_index()
 
     turned = jnp.transpose(fields, (2, 0, 1)).reshape(chan_count, pixels)
-    turned = jnp.pad(turned, ((0, held - chan_count), (0, 0))).reshape(devices, chan, pixels)
-    arrived = lax.all_to_all(turned, AXES, split_axis=0, concat_axis=0, tiled=True)
+    turned = jnp.pad(turned, ((0, active * chan - chan_count), (0, 0)))
+    turned = turned.reshape(active, chan, pixels)
 
     starts = jnp.cumsum(group_size) - group_size
     channel = jnp.arange(held, dtype=jnp.int32)
@@ -147,15 +268,37 @@
     middle = jnp.dot(centre, local.T, precision=lax.Precision.HIGHEST)
     offset = values - middle[:, None, :]
     squares = jnp.dot(jnp.sum(offset * offset, axis=1), local, precision=lax.Precision.HIGHEST)
+    count = row_count * groups
     report = jnp.concatenate(
         [centre.reshape(-1), squares.reshape(-1), band_of_row.astype(jnp.float32)]
     )
-    reports = lax.all_gather(report, AXES, axis=0, tiled=False)
-    count = row_count * groups
+    report = jnp.pad(report, (0, round_up(report.shape[0], 128) - report.shape[0])).reshape(1, -1)
+
+    coef = jnp.pad(basis_coef, ((0, held - chan_count), (0, 0)))
+    coef = lax.dynamic_slice_in_dim(coef, me * chan, chan, axis=0)
+    high = coef.astype(jnp.bfloat16)
+    low = (coef - high.astype(jnp.float32)).astype(jnp.bfloat16)
+    coef = jnp.concatenate([high, low, high], axis=1)
+    basis = basis_spectra.reshape(band_count * TAPS, basis_count, 2, freq_count)
+    arrived, reports, kern = pl.pallas_call(
+        functools.partial(scatter_body, devices, active, freq_count),
+        out_shape=[
+            jax.ShapeDtypeStruct((devices, chan, pixels), jnp.bfloat16),
+            jax.ShapeDtypeStruct((devices, 1, report.shape[1]), jnp.float32),
+            jax.ShapeDtypeStruct((band_count * TAPS, 2 * chan, bins), jnp.float32),
+        ],
+        in_specs=[VMEM] * 4,
+        out_specs=[VMEM] * 3,
+        scratch_shapes=[DMA] * 5,
+        compiler_params=pltpu.CompilerParams(
+            collective_id=0, has_side_effects=True, vmem_limit_bytes=60 * 1024 * 1024
+        ),
+    )(turned, report, coef, basis)
+    reports = reports[:, 0]
     centres = reports[:, :count].reshape(bands, pieces, row_count, groups)
     spreads = reports[:, count : 2 * count].reshape(bands, pieces, row_count, groups)
-    band_rows = reports[:, 2 * count :].reshape(bands, pieces, row_count)[:, 0].reshape(-1)
-    band_rows = band_rows.astype(jnp.int32)
+    band_rows = reports[:, 2 * count : 2 * count + row_count]
+    band_rows = band_rows.reshape(bands, pieces, row_count)[:, 0].reshape(-1).astype(jnp.int32)
     mean = jnp.mean(centres, axis=1)
     total = jnp.sum(spreads + amount * (centres - mean[:, None]) ** 2, axis=1)
     scale = lax.rsqrt(total / (amount * pieces) + EPSILON)
@@ -164,27 +307,7 @@
     mean = pick(mean, mine).reshape(lat_count * chan, 1)
     scale = pick(scale, mine).reshape(lat_count * chan, 1)
 
-    coef = jnp.pad(basis_coef, ((0, held - chan_count), (0, 0)))
-    coef = lax.dynamic_slice_in_dim(coef, me * chan, chan, axis=0)
-    coef = jnp.einsum("cb,pq->pcbq", coef, jnp.eye(2, dtype=jnp.float32))
-    coef = coef.reshape(2 * chan, 2 * basis_count)
-    high = coef.astype(jnp.bfloat16)
-    low = (coef - high.astype(jnp.float32)).astype(jnp.bfloat16)
-    coef = jnp.concatenate([high, low, high], axis=1)
-    basis = basis_spectra.reshape(band_count * TAPS, 2 * basis_count, freq_count)
-    basis = jnp.pad(basis, ((0, 0), (0, 0), (0, bins - freq_count)))
-    kern = pl.pallas_call(
-        kernel_body,
-        out_shape=jax.ShapeDtypeStruct((band_count * TAPS, 2 * chan, bins), jnp.float32),
-        in_specs=[VMEM] * 2,
-        out_specs=VMEM,
-        compiler_params=PARAMS,
-        cost_estimate=pl.CostEstimate(
-            flops=2 * 72 * 48 * 48 * 384, bytes_accessed=10_000_000, transcendentals=0
-        ),
-    )(coef, basis)
-
-    forward, inverse, sums = dft_tables(lon_count, pieces, width, bins)
+    table, sums, weight = dft_tables(lon_count, pieces, width, bins)
     mixed = pl.pallas_call(
         functools.partial(corr_body, pieces, row_count, col_count, width, bins),
         out_shape=jax.ShapeDtypeStruct((devices, chan, pixels), jnp.bfloat16),
@@ -197,9 +320,18 @@
             pltpu.VMEM((lat_count * chan, pieces * width), jnp.float32),
         ],
         compiler_params=PARAMS,
-    )(band_rows, arrived, forward, inverse, sums, mean, scale, kern)
-    returned = lax.all_to_all(mixed, AXES, split_axis=0, concat_axis=0, tiled=True)
-    inputs = returned.reshape(held, pixels)[:chan_count].T.astype(jnp.float32)
+    )(band_rows, arrived, table, sums, weight, mean, scale, kern)
+    returned = pl.pallas_call(
+        functools.partial(gather_body, devices, active),
+        out_shape=jax.ShapeDtypeStruct((active, chan, pixels), jnp.bfloat16),
+        in_specs=[VMEM],
+        out_specs=VMEM,
+        scratch_shapes=[DMA] * 3,
+        compiler_params=pltpu.CompilerParams(
+            collective_id=1, has_side_effects=True, vmem_limit_bytes=60 * 1024 * 1024
+        ),
+    )(mixed)
+    inputs = returned.reshape(active * chan, pixels)[:chan_count].T.astype(jnp.float32)
     centre = jnp.mean(inputs, axis=-1, keepdims=True)
     spread = jnp.mean((inputs - centre) ** 2, axis=-1, keepdims=True)
     normalised = ((inputs - centre) * lax.rsqrt(spread + EPSILON) * mlp_gain).astype(jnp.bfloat16)

time: 113 us -> 79.4 us (0.70)
  blocking collectives: 62.9 us -> 0 us
  Pallas kernels: 15.4 us -> 50.1 us
  starting transfers between devices: 7.33 us -> 0 us
  other arithmetic: 2.32 us -> 9.58 us
  local copies, waits for them, and re-layouts: 16.1 us -> 10 us
    unnamed x1 -> x0, blocking collectives: 40.9 us -> none
    pallas_call x1 -> x2, Pallas kernels: 7.18 us -> 42.3 us  [the longest x1 23.7 us: per_device(): pl.pallas_call(functools.partial(scatter_body, devices, active, freq_coun...]
    all_to_all x1 -> x0, blocking collectives: 22 us -> none  [per_device(): lax.all_to_all(mixed, AXES, split_axis=0, concat_axis=0, tiled=True)]
    all_to_all x1 -> x0, starting transfers between devices: 7.33 us -> none  [per_device(): lax.all_to_all(turned, AXES, split_axis=0, concat_axis=0, tiled=True)]
    pad x2 -> x1, local copies, waits for them, and re-layouts: 3.72 us -> 0.84 us  [per_device(): turned = jnp.pad(turned, ((0, active * chan - chan_count), (0, 0)))]
    reshape x4 -> x1, local copies, waits for them, and re-layouts: 3.61 us -> 0.79 us  [per_device(): band_rows.reshape(bands, pieces, row_count)[:, 0].reshape(-1)]
    unnamed x17 -> x9, local copies, waits for them, and re-layouts: 3.5 us -> 2.49 us
  transfers between devices with their start and end apart: 1 -> 0, of which waited for: 0 -> 0; matrix products, arithmetic and copies ran while one was open for 11% -> 0% of each run, Pallas kernels for 6% -> 0%
where the time goes in v2:
time: 79.4 us; the launch traced here: 78.8 us
  Pallas kernels  50.1 us (63%)
  local copies, waits for them, and re-layouts  10 us (13%)
  other arithmetic  9.58 us (12%)
  matrix products  8.92 us (11%)
    pallas_call x1, Pallas kernels, per_device(): pl.pallas_call(functools.partial(scatter_body, devices, active, freq_coun...  23.7 us
    pallas_call x1, Pallas kernels, per_device(): pl.pallas_call(functools.partial(gather_body, devices, active), out_shape...  18.6 us
    dot_general x1, matrix products, per_device(): result = inputs + jnp.dot(hidden, w_out, preferred_element_type=jnp.float32)  8.09 us
    pallas_call x1, Pallas kernels, per_device(): pl.pallas_call(functools.partial(corr_body, pieces, row_count, col_count,...  7.87 us
    unnamed x9, local copies, waits for them, and re-layouts  2.49 us
    reshape x2, local copies, waits for them, and re-layouts, per_device(): return result.astype(jnp.bfloat16).reshape(row_count, col_count, chan_count)  2.39 us

profile of v2, /device:TPU:0, one launch (start us, length us, event | category | flops | bytes accessed | tf_op | source)
XLA Modules:
  0.0 78.8 jit_solution(11556994264583536577)
XLA Ops:
  0.0 0.0 copy-start
  0.0 0.0 copy-start.1
  0.0 1.0 %reduce-window.8 = s32[8,1]{0,1:T(1,128)S(1)} reduce-window(s32[8,1]{0,1:T(1,128)} %bitcast.58, s32[]{:T(128)} %constant.47.clone.1), window={size=8x1 pad=7_0x0_0}, to_apply=%region_1.2 | reduce-window | flops 56 | bytes 68 | tf_op jit(solution)/shard_map/reduce-window.3
  1.0 0.7 bitcast_subtract_fusion
  1.6 0.7 convert_element_type.47
  2.3 0.7 convert_multiply_fusion
  3.0 0.1 fusion.63
  3.0 1.3 %convert_reduce_fusion = f32[4,641]{1,0:T(4,128)S(1)} fusion(bf16[4,90,641]{2,0,1:T(4,128)(2,1)} %param.11), kind=kLoop, calls=%fused_computation.20 | loop fusion | flops 458956 | bytes 471776 | tf_op jit(solution)/shard_map/reduce_sum | solution.py:266
  4.4 0.1 convolution_divide_fusion
  4.5 0.1 reshape.88
  4.6 0.2 fusion.66
  4.7 1.5 %fusion.15 = f32[4,641]{1,0:T(4,128)S(1)} fusion(bf16[4,90,641]{2,0,1:T(4,128)(2,1)} %param.11, f32[4,641]{1,0:T(4,128)S(1)} %fusion.66), kind=kLoop, calls=%fused_computation.30 | loop fusion | flops 920476 | bytes 482032 | tf_op jit(solution)/shard_map/reduce_sum | solution.py:270
  6.2 0.1 fusion.64
  6.3 0.1 reshape.89
  6.4 0.6 fusion.80.report_ref
  7.0 0.9 %copy.27 = f32[641,8]{1,0:T(8,128)S(1)} copy(f32[641,8]{0,1:T(8,128)} %param.15) | data formatting | bytes 41024 | tf_op args[4]
  7.9 0.7 pad_maximum_fusion.coef_ref
  8.6 0.0 copy-done.1
  8.6 0.9 %copy.40 = bf16[641,4,90]{2,1,0:T(4,128)(2,1)S(1)} copy(bf16[641,4,90]{0,1,2:T(4,128)(2,1)S(1)} %bitcast.48) | data formatting | bytes 923040
  9.6 0.7 reshape.103
  10.2 0.8 %pad.12.clone = bf16[648,360]{1,0:T(8,128)(2,1)} pad(bf16[641,360]{1,0:T(8,128)(2,1)S(1)} %reshape.103, bf16[]{:T(256)} %constant.45.clone.1), padding=0_7x0_0 | pad | bytes 928082 | tf_op jit(solution)/shard_map/jit(_pad)/pad | solution.py:253
  11.0 23.7 %shard_map.109 = (bf16[32,24,360]{2,1,0:T(8,128)(2,1)}, f32[32,1,128]{2,1,0:T(1,128)}, f32[72,48,384]{2,1,0:T(8,128)}) custom-call(bf16[27,24,360]{2,1,0:T(8,128)(2,1)} %bitcast.52, f32[1,128]{1,0:T(1,128)} %fusion.80.report_ref, bf16[24,24]{1,0:T(8,128)(2,1)} %pad_maximum_fusion.coef_ref, f32[72,8,2,361]{3,2,1,0:T(2,128)} %bitcast.53), custom_call_target="tpu_custom_call" | custom-call | tf_op jit(solution)/shard_map/pallas_call | solution.py:283
  34.8 0.8 %slice_bitcast_fusion = f32[4,8,4]{2,1,0:T(8,128)S(1)} fusion(f32[32,128]{1,0:T(8,128)} %bitcast.54), kind=kLoop, calls=%fused_computation.73 | loop fusion | bytes 1024 | tf_op jit(solution)/shard_map/reshape | solution.py:301
  35.6 0.7 convert_element_type.52.band_ref
  36.3 0.9 %fusion.114 = (f32[32,32]{1,0:T(8,128)S(1)}, f32[32,32]{1,0:T(8,128)S(1)}) fusion(f32[32,128]{1,0:T(8,128)} %bitcast.55), kind=kLoop, calls=%fused_computation.135 | loop fusion | bytes 16384 | tf_op jit(solution)/shard_map/slice | solution.py:299
  37.1 0.1 reshape.95
  37.2 0.1 reshape.93
  37.3 0.2 fusion.76
  37.6 0.2 fusion.69
  37.8 0.8 %reshape.101.scale_ref = f32[384,1]{1,0:T(8,128)} reshape(f32[4,4,24]{2,1,0:T(4,128)S(1)} %fusion.69) | data formatting | bytes 3072 | tf_op jit(solution)/shard_map/reshape | solution.py:308
  38.6 0.8 %reshape.100.mean_ref = f32[384,1]{1,0:T(8,128)} reshape(f32[4,4,24]{2,1,0:T(4,128)S(1)} %fusion.76) | data formatting | bytes 3072 | tf_op jit(solution)/shard_map/reshape | solution.py:307
  39.4 7.9 %shard_map.110.mixed_ref = bf16[32,24,360]{2,1,0:T(8,128)(2,1)} custom-call(s32[16]{0:T(128)} %convert_element_type.52.band_ref, bf16[32,24,360]{2,1,0:T(8,128)(2,1)} %get-tuple-element.9.block_ref, bf16[1024,768]{1,0:T(8,128)(2,1)} %constant.104.clone.table_ref, f32[1,768]{1,0:T(1,128)} %constant.105.clone.total_ref, f32[1,768]{1,0:T(1,128)} %constant.106.clone.weight_ref, ...), custom_call_target="tpu_custom_call" | custom-call | tf_op jit(solution)/shard_map/pallas_call | solution.py:311
  47.3 0.0 copy-start.2
  47.3 18.6 %shard_map.111 = bf16[27,24,360]{2,1,0:T(8,128)(2,1)} custom-call(bf16[32,24,360]{2,1,0:T(8,128)(2,1)} %shard_map.110.mixed_ref), custom_call_target="tpu_custom_call" | custom-call | tf_op jit(solution)/shard_map/pallas_call | solution.py:324
  65.9 1.2 %convert_reduce_fusion.1 = f32[360]{0:T(512)S(1)} fusion(bf16[648,360]{1,0:T(8,128)(2,1)} %bitcast.49), kind=kLoop, calls=%fused_computation.23 | loop fusion | flops 461160 | bytes 462960 | tf_op jit(solution)/shard_map/reduce_sum | solution.py:335
  67.0 1.2 %fusion.16 = f32[360]{0:T(512)S(1)} fusion(f32[360]{0:T(512)S(1)} %broadcast_multiply_fusion.1, bf16[648,360]{1,0:T(8,128)(2,1)} %bitcast.50), kind=kLoop, calls=%fused_computation.31 | loop fusion | flops 922680 | bytes 464400 | tf_op jit(solution)/shard_map/reduce_sum | solution.py:336
  68.3 0.0 copy-done
  68.3 0.0 copy-done.2
  68.3 8.1 %fusion.10 = bf16[360,641]{0,1:T(8,128)(2,1)S(1)} fusion(bf16[1282,641]{0,1:T(8,128)(2,1)S(1)} %copy-done, bf16[641,1282]{1,0:T(8,128)(2,1)} %param.17, f32[641]{0:T(1024)S(1)} %copy-done.2, f32[360]{0:T(512)S(1)} %add_rsqrt_fusion, f32[360]{0:T(512)S(1)} %broadcast_multiply_fusion.1, bf16[648,360]{1,0:T(8,128)(2,1)} %bitcast.51), kind=kOutput, calls=%fused_computation.22 | convolution fusion | flops 1215181056 | bytes 4930584 | tf_op jit(solution)/shard_map/dot_general | solution.py:341
  76.4 0.8 %reshape.102 = bf16[4,90,641]{1,0,2:T(4,128)(2,1)S(1)} reshape(bf16[360,641]{0,1:T(8,128)(2,1)S(1)} %fusion.10) | data formatting | bytes 923040 | tf_op jit(solution)/shard_map/reshape | solution.py:342
  77.2 1.6 %copy.33 = bf16[4,90,641]{2,0,1:T(4,128)(2,1)} copy(bf16[4,90,641]{1,0,2:T(4,128)(2,1)S(1)} %reshape.102) | data formatting | bytes 923040 | tf_op jit(solution)/shard_map/reshape | solution.py:342
  (8 shorter events, 0.1 us)
Async XLA Ops:
  0.0 68.3 %copy-start = (bf16[1282,641]{0,1:T(8,128)(2,1)S(1)}, bf16[1282,641]{0,1:T(8,128)(2,1)}, u32[]{:S(2)}) copy-start(bf16[1282,641]{0,1:T(8,128)(2,1)} %param.18) | copy-start | bytes 4930576
  0.0 8.6 %copy-start.1 = (bf16[4,90,641]{2,0,1:T(4,128)(2,1)S(1)}, bf16[4,90,641]{2,0,1:T(4,128)(2,1)}, u32[]{:S(2)}) copy-start(bf16[4,90,641]{2,0,1:T(4,128)(2,1)} %param.11) | copy-start | bytes 1384564
  47.3 21.0 %copy-start.2 = (f32[641]{0:T(1024)S(1)}, f32[641]{0:T(1024)}, u32[]{:S(2)}) copy-start(f32[641]{0:T(1024)} %param.16) | copy-start | bytes 7696

commit v3 on v2

--- a/solution.py
+++ b/solution.py
@@ -69,10 +69,26 @@
     pltpu.make_async_copy(part, part, semaphore).wait()
 
 
+def group_rows(size_ref, lanes, groups):
+    group = lax.rem(lax.broadcasted_iota(jnp.int32, (1, lanes), 1), groups)
+    start = jnp.zeros((1, lanes), jnp.int32)
+    size = jnp.zeros((1, lanes), jnp.int32)
+    for index in range(groups):
+        start = start + jnp.where(group > index, size_ref[index], 0)
+        size = size + jnp.where(group == index, size_ref[index], 0)
+    return start, size
+
+
+def membership(first, chan, start, size):
+    channel = first + lax.broadcasted_iota(jnp.int32, (chan, start.shape[1]), 0)
+    return (channel >= start) & (channel < start + size)
+
+
 def scatter_body(
-    devices, active, freq,
-    block_ref, report_ref, coef_ref, basis_ref,
+    devices, active, freq, rows, cols, groups,
+    size_ref, band_ref, block_ref, coef_ref, basis_ref,
     arrived_ref, reports_ref, kern_ref,
+    mean_ref, square_ref, report_ref,
     send_sem, recv_sem, report_send_sem, report_recv_sem, local_sem,
 ):
     me = own_index()
@@ -80,14 +96,6 @@
 
     def send(step, carry):
         target = lax.rem(me + step, devices)
-        pltpu.make_async_remote_copy(
-            src_ref=report_ref,
-            dst_ref=reports_ref.at[me],
-            send_sem=report_send_sem,
-            recv_sem=report_recv_sem,
-            device_id=place(target),
-            device_id_type=MESH,
-        ).start()
 
         @pl.when(target < active)
         def _():
@@ -103,14 +111,68 @@
         return carry
 
     lax.fori_loop(1, devices, send, 0)
-    reports_ref[me] = report_ref[...]
     own = pltpu.make_async_copy(
         block_ref.at[lax.rem(me, active)], arrived_ref.at[me], local_sem
     )
     own.start()
 
-    chan, bins = kern_ref.shape[1] // 2, kern_ref.shape[2]
-    coef = coef_ref[...]
+    chan = block_ref.shape[1]
+    lane = lax.broadcasted_iota(jnp.int32, (chan, block_ref.shape[2]), 1)
+    slot = lax.broadcasted_iota(jnp.int32, (chan, 128), 1)
+
+    def measure(n, carry):
+        cells = block_ref[n].astype(jnp.float32)
+        means = jnp.zeros((chan, 128), jnp.float32)
+        squares = jnp.zeros((chan, 128), jnp.float32)
+        for row in range(rows):
+            inside = (lane >= row * cols) & (lane < (row + 1) * cols)
+            mean = jnp.sum(jnp.where(inside, cells, 0.0), axis=1, keepdims=True) / cols
+            offset = jnp.where(inside, cells - mean, 0.0)
+            square = jnp.sum(offset * offset, axis=1, keepdims=True)
+            means = jnp.where(slot == row, mean, means)
+            squares = jnp.where(slot == row, square, squares)
+        at = pl.multiple_of(n * chan, 8)
+        mean_ref[pl.ds(at, chan)] = means
+        square_ref[pl.ds(at, chan)] = squares
+        return carry
+
+    lax.fori_loop(0, active, measure, 0)
+    exact = functools.partial(
+        lax.dot_general, precision=lax.Precision.HIGHEST, preferred_element_type=jnp.float32
+    )
+    over_chan = (((0,), (0,)), ((), ()))
+    over_last = (((1,), (1,)), ((), ()))
+    start, size = group_rows(size_ref, 128, groups)
+    member = jnp.where(
+        membership(0, active * chan, start, size)
+        & (lax.broadcasted_iota(jnp.int32, (1, 128), 1) < groups),
+        1.0, 0.0,
+    )
+    means = mean_ref[...]
+    centre = exact(means, member, over_chan) / jnp.maximum(size, 1).astype(jnp.float32)
+    offset = means - exact(member, centre, over_last)
+    spread = exact(square_ref[...] + cols * offset * offset, member, over_chan)
+    rest = report_ref.shape[1] - 2 * rows * groups
+    place_of = lax.broadcasted_iota(jnp.int32, (1, rest), 1)
+    bands = jnp.zeros((1, rest), jnp.float32)
+    for row in range(rows):
+        bands = jnp.where(place_of == row, band_ref[row].astype(jnp.float32), bands)
+    report = jnp.concatenate(
+        [centre[row : row + 1, :groups] for row in range(rows)]
+        + [spread[row : row + 1, :groups] for row in range(rows)]
+        + [bands],
+        axis=1,
+    )
+    report_ref[...] = report
+    reports_ref[me] = report
+
+    bins = kern_ref.shape[2]
+    total = coef_ref.shape[1]
+    wanted = me * chan + lax.broadcasted_iota(jnp.int32, (chan, total), 0)
+    chosen = jnp.where(lax.broadcasted_iota(jnp.int32, (chan, total), 1) == wanted, 1.0, 0.0)
+    coef = exact(chosen, coef_ref[...], over_last)
+    high = coef.astype(jnp.bfloat16).astype(jnp.float32)
+    coef = jnp.concatenate([high, coef - high, high], axis=1).astype(jnp.bfloat16)
     blank = jnp.zeros((basis_ref.shape[1], bins - freq), jnp.float32)
 
     def generate(n, carry):
@@ -123,7 +185,21 @@
             )
         return carry
 
-    lax.fori_loop(0, basis_ref.shape[0], generate, 0)
+    def tell(step, carry):
+        pltpu.make_async_remote_copy(
+            src_ref=report_ref,
+            dst_ref=reports_ref.at[me],
+            send_sem=report_send_sem,
+            recv_sem=report_recv_sem,
+            device_id=place(lax.rem(me + step, devices)),
+            device_id_type=MESH,
+        ).start()
+        return carry
+
+    early = basis_ref.shape[0] // 8
+    lax.fori_loop(0, early, generate, 0)
+    lax.fori_loop(1, devices, tell, 0)
+    lax.fori_loop(early, basis_ref.shape[0], generate, 0)
     own.wait()
     drain(reports_ref, devices - 1, report_send_sem)
     drain(reports_ref, devices - 1, report_recv_sem)
@@ -175,13 +251,39 @@
 
 
 def corr_body(
-    pieces, rows, cols, width, bins,
-    band_ref, block_ref, table_ref, total_ref, weight_ref, mean_ref, scale_ref, kern_ref,
+    pieces, rows, cols, width, bins, groups,
+    size_ref, block_ref, reports_ref, table_ref, total_ref, weight_ref, kern_ref,
     out_ref, wide_ref, spec_ref, prod_ref, corr_ref,
 ):
     chan = block_ref.shape[1]
     bands = block_ref.shape[0] // pieces
     lat = bands * rows
+    lanes = reports_ref.shape[2]
+    start, size = group_rows(size_ref, lanes, groups)
+    amount = size.astype(jnp.float32) * cols
+    lane = lax.broadcasted_iota(jnp.int32, (1, lanes), 1)
+    member = membership(own_index() * chan, chan, start, size)
+    means, scales, numbers = [], [], []
+    for band in range(bands):
+        report = reports_ref[band * pieces : (band + 1) * pieces, 0]
+        centre = jnp.sum(report, axis=0, keepdims=True) / pieces
+        offset = report - centre
+        between = amount * jnp.sum(offset * offset, axis=0, keepdims=True)
+        within = jnp.sum(report, axis=0, keepdims=True)
+        for row in range(rows):
+            low, high = row * groups, (rows + row) * groups
+            here = member & (lane >= low) & (lane < low + groups)
+            there = member & (lane >= high) & (lane < high + groups)
+
+            def pick(mask, cells):
+                return jnp.sum(jnp.where(mask, cells, 0.0), axis=1, keepdims=True)
+
+            square = pick(here, between) + pick(there, within)
+            count = pick(here, amount) * pieces
+            means.append(pick(here, centre))
+            scales.append(lax.rsqrt(square / jnp.maximum(count, 1.0) + EPSILON))
+            mark = lane == 2 * rows * groups + row
+            numbers.append(jnp.sum(jnp.where(mark, report[:1], 0.0)).astype(jnp.int32))
     wide_ref[...] = jnp.zeros_like(wide_ref)
     for band in range(bands):
         for piece in range(pieces):
@@ -194,9 +296,11 @@
     raw = jnp.dot(
         wide_ref[...].astype(jnp.bfloat16), table_ref[...], preferred_element_type=jnp.float32
     )
-    spec_ref[...] = (raw - mean_ref[...] * total_ref[...]) * scale_ref[...]
     for row in range(lat):
-        band = band_ref[row]
+        at = row * chan
+        spec_ref[at : at + chan] = (raw[at : at + chan] - means[row] * total_ref[...]) * scales[row]
+    for row in range(lat):
+        band = numbers[row]
         real = jnp.zeros((chan, bins), jnp.float32)
         imag = jnp.zeros((chan, bins), jnp.float32)
         for tap in range(TAPS):
@@ -242,76 +346,43 @@
     groups = group_size.shape[0]
     pixels = row_count * col_count
     chan = round_up(-(-chan_count // devices), 8)
-    held = devices * chan
     active = -(-chan_count // chan)
     width = round_up(col_count, 128)
     bins = round_up(freq_count, 128)
     band_count, _, basis_count = basis_spectra.shape[:3]
-    me = own_index()
 
     turned = jnp.transpose(fields, (2, 0, 1)).reshape(chan_count, pixels)
     turned = jnp.pad(turned, ((0, active * chan - chan_count), (0, 0)))
     turned = turned.reshape(active, chan, pixels)
 
-    starts = jnp.cumsum(group_size) - group_size
-    channel = jnp.arange(held, dtype=jnp.int32)
-    within = (channel[:, None] >= starts[None, :]) & (
-        channel[:, None] < (starts + group_size)[None, :]
-    )
-    member = within.astype(jnp.float32)
-    local = member[:chan_count]
-    values = fields.astype(jnp.float32)
-    amount = group_size.astype(jnp.float32) * col_count
-    centre = (
-        jnp.dot(jnp.sum(values, axis=1), local, precision=lax.Precision.HIGHEST) / amount
-    )
-    middle = jnp.dot(centre, local.T, precision=lax.Precision.HIGHEST)
-    offset = values - middle[:, None, :]
-    squares = jnp.dot(jnp.sum(offset * offset, axis=1), local, precision=lax.Precision.HIGHEST)
-    count = row_count * groups
-    report = jnp.concatenate(
-        [centre.reshape(-1), squares.reshape(-1), band_of_row.astype(jnp.float32)]
-    )
-    report = jnp.pad(report, (0, round_up(report.shape[0], 128) - report.shape[0])).reshape(1, -1)
-
-    coef = jnp.pad(basis_coef, ((0, held - chan_count), (0, 0)))
-    coef = lax.dynamic_slice_in_dim(coef, me * chan, chan, axis=0)
-    high = coef.astype(jnp.bfloat16)
-    low = (coef - high.astype(jnp.float32)).astype(jnp.bfloat16)
-    coef = jnp.concatenate([high, low, high], axis=1)
+    lanes = round_up((2 * groups + 1) * row_count, 128)
     basis = basis_spectra.reshape(band_count * TAPS, basis_count, 2, freq_count)
     arrived, reports, kern = pl.pallas_call(
-        functools.partial(scatter_body, devices, active, freq_count),
+        functools.partial(
+            scatter_body, devices, active, freq_count, row_count, col_count, groups
+        ),
         out_shape=[
             jax.ShapeDtypeStruct((devices, chan, pixels), jnp.bfloat16),
-            jax.ShapeDtypeStruct((devices, 1, report.shape[1]), jnp.float32),
+            jax.ShapeDtypeStruct((devices, 1, lanes), jnp.float32),
             jax.ShapeDtypeStruct((band_count * TAPS, 2 * chan, bins), jnp.float32),
         ],
-        in_specs=[VMEM] * 4,
+        in_specs=[SMEM] * 2 + [VMEM] * 3,
         out_specs=[VMEM] * 3,
-        scratch_shapes=[DMA] * 5,
+        scratch_shapes=[
+            pltpu.VMEM((active * chan, 128), jnp.float32),
+            pltpu.VMEM((active * chan, 128), jnp.float32),
+            pltpu.VMEM((1, lanes), jnp.float32),
+        ]
+        + [DMA] * 5,
         compiler_params=pltpu.CompilerParams(
             collective_id=0, has_side_effects=True, vmem_limit_bytes=60 * 1024 * 1024
         ),
-    )(turned, report, coef, basis)
-    reports = reports[:, 0]
-    centres = reports[:, :count].reshape(bands, pieces, row_count, groups)
-    spreads = reports[:, count : 2 * count].reshape(bands, pieces, row_count, groups)
-    band_rows = reports[:, 2 * count : 2 * count + row_count]
-    band_rows = band_rows.reshape(bands, pieces, row_count)[:, 0].reshape(-1).astype(jnp.int32)
-    mean = jnp.mean(centres, axis=1)
-    total = jnp.sum(spreads + amount * (centres - mean[:, None]) ** 2, axis=1)
-    scale = lax.rsqrt(total / (amount * pieces) + EPSILON)
-    mine = lax.dynamic_slice_in_dim(member, me * chan, chan, axis=0)
-    pick = functools.partial(jnp.einsum, "irg,cg->irc", precision=lax.Precision.HIGHEST)
-    mean = pick(mean, mine).reshape(lat_count * chan, 1)
-    scale = pick(scale, mine).reshape(lat_count * chan, 1)
-
+    )(group_size, band_of_row, turned, basis_coef.T, basis)
     table, sums, weight = dft_tables(lon_count, pieces, width, bins)
     mixed = pl.pallas_call(
-        functools.partial(corr_body, pieces, row_count, col_count, width, bins),
+        functools.partial(corr_body, pieces, row_count, col_count, width, bins, groups),
         out_shape=jax.ShapeDtypeStruct((devices, chan, pixels), jnp.bfloat16),
-        in_specs=[SMEM] + [VMEM] * 7,
+        in_specs=[SMEM] + [VMEM] * 6,
         out_specs=VMEM,
         scratch_shapes=[
             pltpu.VMEM((lat_count * chan, pieces * width), jnp.float32),
@@ -320,7 +391,7 @@
             pltpu.VMEM((lat_count * chan, pieces * width), jnp.float32),
         ],
         compiler_params=PARAMS,
-    )(band_rows, arrived, table, sums, weight, mean, scale, kern)
+    )(group_size, arrived, reports, table, sums, weight, kern)
     returned = pl.pallas_call(
         functools.partial(gather_body, devices, active),
         out_shape=jax.ShapeDtypeStruct((active, chan, pixels), jnp.bfloat16),

time: 79.4 us -> 71.6 us (0.902)
  other arithmetic: 9.58 us -> 2.38 us
  Pallas kernels: 50.1 us -> 54.9 us
  local copies, waits for them, and re-layouts: 10 us -> 5.84 us
  matrix products: 8.92 us -> 8.08 us
    pallas_call x1, Pallas kernels: 23.7 us -> 29.1 us  [per_device(): pl.pallas_call(functools.partial(scatter_body, devices, active, freq_coun...]
    reduce_sum x4 -> x0, other arithmetic: 2.85 us -> none  [the longest x1 1.46 us: per_device(): jnp.sum(offset * offset, axis=1)]
    reshape x7 -> x0, local copies, waits for them, and re-layouts: 2.74 us -> none  [the longest x1 0.8 us: per_device(): mean = pick(mean, mine).reshape(lat_count * chan, 1)]
    another operation x1 -> x0, other arithmetic: 0.98 us -> none
    slice x2 -> x0, local copies, waits for them, and re-layouts: 0.87 us -> none  [the longest x1 0.86 us: per_device(): reports[:, count:2 * count].reshape(bands, pieces, row_count, groups)]
    dot_general x5 -> x0, matrix products: 0.83 us -> none  [the longest x1 0.22 us: per_device(): mean = pick(mean, mine).reshape(lat_count * chan, 1)]
    unnamed x9 -> x6, local copies, waits for them, and re-layouts: 2.49 us -> 2.61 us
where the time goes in v3:
time: 71.6 us; the launch traced here: 71.3 us
  Pallas kernels  54.9 us (77%)
  matrix products  8.08 us (11%)
  local copies, waits for them, and re-layouts  5.84 us (8%)
  other arithmetic  2.38 us (3%)
    pallas_call x1, Pallas kernels, per_device(): pl.pallas_call(functools.partial(scatter_body, devices, active, freq_coun...  29.1 us
    pallas_call x1, Pallas kernels, per_device(): pl.pallas_call(functools.partial(gather_body, devices, active), out_shape...  18.1 us
    dot_general x1, matrix products, per_device(): result = inputs + jnp.dot(hidden, w_out, preferred_element_type=jnp.float32)  8.08 us
    pallas_call x1, Pallas kernels, per_device(): pl.pallas_call(functools.partial(corr_body, pieces, row_count, col_count,...  7.75 us
    unnamed x6, local copies, waits for them, and re-layouts  2.61 us
    reshape x2, local copies, waits for them, and re-layouts, per_device(): return result.astype(jnp.bfloat16).reshape(row_count, col_count, chan_count)  2.39 us

profile of v3, /device:TPU:0, one launch (start us, length us, event | category | flops | bytes accessed | tf_op | source)
XLA Modules:
  0.0 71.3 jit_solution(5037759510492545281)
XLA Ops:
  0.0 0.0 copy-start
  0.0 1.9 %copy.20 = bf16[641,4,90]{2,1,0:T(4,128)(2,1)S(1)} copy(bf16[641,4,90]{0,1,2:T(4,128)(2,1)} %bitcast.35) | data formatting | bytes 923040
  2.0 0.7 reshape.34
  2.6 0.8 %pad.4.clone = bf16[648,360]{1,0:T(8,128)(2,1)} pad(bf16[641,360]{1,0:T(8,128)(2,1)S(1)} %reshape.34, bf16[]{:T(256)} %constant.36.clone.1), padding=0_7x0_0 | pad | bytes 928082 | tf_op jit(solution)/shard_map/jit(_pad)/pad | solution.py:355
  3.5 29.1 %shard_map.109 = (bf16[32,24,360]{2,1,0:T(8,128)(2,1)}, f32[32,1,128]{2,1,0:T(1,128)}, f32[72,48,384]{2,1,0:T(8,128)}) custom-call(s32[8]{0:T(128)} %size_ref.3, s32[4]{0:T(128)} %band_ref.1, bf16[27,24,360]{2,1,0:T(8,128)(2,1)} %bitcast.33, f32[8,641]{1,0:T(8,128)} %bitcast.36, f32[72,8,2,361]{3,2,1,0:T(2,128)} %bitcast.34), custom_call_target="tpu_custom_call" | custom-call | tf_op jit(solution)/shard_map/pallas_call | solution.py:360
  32.5 7.8 %shard_map.110.mixed_ref = bf16[32,24,360]{2,1,0:T(8,128)(2,1)} custom-call(s32[8]{0:T(128)} %size_ref.3, bf16[32,24,360]{2,1,0:T(8,128)(2,1)} %get-tuple-element.8.block_ref, f32[32,1,128]{2,1,0:T(1,128)} %get-tuple-element.9.reports_ref, bf16[1024,768]{1,0:T(8,128)(2,1)} %constant.76.clone.table_ref, f32[1,768]{1,0:T(1,128)} %constant.77.clone.total_ref, ...), custom_call_target="tpu_custom_call" | custom-call | tf_op jit(solution)/shard_map/pallas_call | solution.py:382
  40.3 0.0 copy-start.1
  40.3 18.1 %shard_map.111 = bf16[27,24,360]{2,1,0:T(8,128)(2,1)} custom-call(bf16[32,24,360]{2,1,0:T(8,128)(2,1)} %shard_map.110.mixed_ref), custom_call_target="tpu_custom_call" | custom-call | tf_op jit(solution)/shard_map/pallas_call | solution.py:395
  58.4 1.2 %convert_reduce_fusion = f32[360]{0:T(512)S(1)} fusion(bf16[648,360]{1,0:T(8,128)(2,1)} %bitcast.30), kind=kLoop, calls=%fused_computation.21 | loop fusion | flops 461160 | bytes 462960 | tf_op jit(solution)/shard_map/reduce_sum | solution.py:406
  59.6 1.2 %fusion.14 = f32[360]{0:T(512)S(1)} fusion(f32[360]{0:T(512)S(1)} %broadcast_multiply_fusion, bf16[648,360]{1,0:T(8,128)(2,1)} %bitcast.31), kind=kLoop, calls=%fused_computation.26 | loop fusion | flops 922680 | bytes 464400 | tf_op jit(solution)/shard_map/reduce_sum | solution.py:407
  60.8 0.0 copy-done
  60.8 0.0 copy-done.1
  60.8 8.1 %fusion.10 = bf16[360,641]{0,1:T(8,128)(2,1)S(1)} fusion(bf16[1282,641]{0,1:T(8,128)(2,1)S(1)} %copy-done, bf16[641,1282]{1,0:T(8,128)(2,1)} %param.17, f32[641]{0:T(1024)S(1)} %copy-done.1, f32[360]{0:T(512)S(1)} %add_rsqrt_fusion, f32[360]{0:T(512)S(1)} %broadcast_multiply_fusion, bf16[648,360]{1,0:T(8,128)(2,1)} %bitcast.32), kind=kOutput, calls=%fused_computation.20 | convolution fusion | flops 1215181056 | bytes 4930584 | tf_op jit(solution)/shard_map/dot_general | solution.py:412
  68.9 0.8 %reshape.33 = bf16[4,90,641]{1,0,2:T(4,128)(2,1)S(1)} reshape(bf16[360,641]{0,1:T(8,128)(2,1)S(1)} %fusion.10) | data formatting | bytes 923040 | tf_op jit(solution)/shard_map/reshape | solution.py:413
  69.7 1.6 %copy.16 = bf16[4,90,641]{2,0,1:T(4,128)(2,1)} copy(bf16[4,90,641]{1,0,2:T(4,128)(2,1)S(1)} %reshape.33) | data formatting | bytes 923040 | tf_op jit(solution)/shard_map/reshape | solution.py:413
  (2 shorter events, 0.0 us)
Async XLA Ops:
  0.0 60.8 %copy-start = (bf16[1282,641]{0,1:T(8,128)(2,1)S(1)}, bf16[1282,641]{0,1:T(8,128)(2,1)}, u32[]{:S(2)}) copy-start(bf16[1282,641]{0,1:T(8,128)(2,1)} %param.18) | copy-start | bytes 4930576
  40.3 20.5 %copy-start.1 = (f32[641]{0:T(1024)S(1)}, f32[641]{0:T(1024)}, u32[]{:S(2)}) copy-start(f32[641]{0:T(1024)} %param.16) | copy-start | bytes 7696

commit v4 on v3

--- a/solution.py
+++ b/solution.py
@@ -86,9 +86,9 @@
 
 def scatter_body(
     devices, active, freq, rows, cols, groups,
-    size_ref, band_ref, block_ref, coef_ref, basis_ref,
+    size_ref, band_ref, block_ref, flat_ref, coef_ref, basis_ref,
     arrived_ref, reports_ref, kern_ref,
-    mean_ref, square_ref, report_ref,
+    report_ref,
     send_sem, recv_sem, report_send_sem, report_recv_sem, local_sem,
 ):
     me = own_index()
@@ -117,26 +117,27 @@
     own.start()
 
     chan = block_ref.shape[1]
-    lane = lax.broadcasted_iota(jnp.int32, (chan, block_ref.shape[2]), 1)
-    slot = lax.broadcasted_iota(jnp.int32, (chan, 128), 1)
-
-    def measure(n, carry):
-        cells = block_ref[n].astype(jnp.float32)
-        means = jnp.zeros((chan, 128), jnp.float32)
-        squares = jnp.zeros((chan, 128), jnp.float32)
-        for row in range(rows):
-            inside = (lane >= row * cols) & (lane < (row + 1) * cols)
-            mean = jnp.sum(jnp.where(inside, cells, 0.0), axis=1, keepdims=True) / cols
-            offset = jnp.where(inside, cells - mean, 0.0)
-            square = jnp.sum(offset * offset, axis=1, keepdims=True)
-            means = jnp.where(slot == row, mean, means)
-            squares = jnp.where(slot == row, square, squares)
-        at = pl.multiple_of(n * chan, 8)
-        mean_ref[pl.ds(at, chan)] = means
-        square_ref[pl.ds(at, chan)] = squares
-        return carry
-
-    lax.fori_loop(0, active, measure, 0)
+    pixels = rows * cols
+    lane = lax.broadcasted_iota(jnp.int32, (pixels, 128), 0)
+    slot = lax.broadcasted_iota(jnp.int32, (pixels, 128), 1)
+    segment = (lane >= slot * cols) & (lane < (slot + 1) * cols)
+    segment = jnp.where(segment, 1.0, 0.0).astype(jnp.bfloat16)
+
+    def add_up(cells):
+        return jnp.dot(cells, segment, preferred_element_type=jnp.float32)
+
+    cells = flat_ref[...]
+    means = add_up(cells) / cols
+    near = means.astype(jnp.bfloat16)
+    spread_out = lax.dot_general(
+        near, segment, (((1,), (1,)), ((), ())), preferred_element_type=jnp.float32
+    )
+    offset = cells.astype(jnp.float32) - spread_out
+    square = offset * offset
+    high = square.astype(jnp.bfloat16)
+    low = (square - high.astype(jnp.float32)).astype(jnp.bfloat16)
+    shift = means - near.astype(jnp.float32)
+    squares = jnp.maximum(add_up(high) + add_up(low) - cols * shift * shift, 0.0)
     exact = functools.partial(
         lax.dot_general, precision=lax.Precision.HIGHEST, preferred_element_type=jnp.float32
     )
@@ -148,10 +149,9 @@
         & (lax.broadcasted_iota(jnp.int32, (1, 128), 1) < groups),
         1.0, 0.0,
     )
-    means = mean_ref[...]
     centre = exact(means, member, over_chan) / jnp.maximum(size, 1).astype(jnp.float32)
     offset = means - exact(member, centre, over_last)
-    spread = exact(square_ref[...] + cols * offset * offset, member, over_chan)
+    spread = exact(squares + cols * offset * offset, member, over_chan)
     rest = report_ref.shape[1] - 2 * rows * groups
     place_of = lax.broadcasted_iota(jnp.int32, (1, rest), 1)
     bands = jnp.zeros((1, rest), jnp.float32)
@@ -176,13 +176,14 @@
     blank = jnp.zeros((basis_ref.shape[1], bins - freq), jnp.float32)
 
     def generate(n, carry):
-        for part in range(2):
-            basis = jnp.concatenate([basis_ref[n, :, part, :], blank], axis=1)
-            high = basis.astype(jnp.bfloat16).astype(jnp.float32)
-            both = jnp.concatenate([high, high, basis - high], axis=0).astype(jnp.bfloat16)
-            kern_ref[n, part * chan : (part + 1) * chan] = jnp.dot(
-                coef, both, preferred_element_type=jnp.float32
-            )
+        basis = jnp.concatenate(
+            [basis_ref[n, :, 0, :], blank, basis_ref[n, :, 1, :], blank], axis=1
+        )
+        high = basis.astype(jnp.bfloat16).astype(jnp.float32)
+        both = jnp.concatenate([high, high, basis - high], axis=0).astype(jnp.bfloat16)
+        made = jnp.dot(coef, both, preferred_element_type=jnp.float32)
+        kern_ref[n, :chan] = made[:, :bins]
+        kern_ref[n, chan:] = made[:, bins:]
         return carry
 
     def tell(step, carry):
@@ -197,9 +198,9 @@
         return carry
 
     early = basis_ref.shape[0] // 8
-    lax.fori_loop(0, early, generate, 0)
+    lax.fori_loop(0, early, generate, 0, unroll=3)
     lax.fori_loop(1, devices, tell, 0)
-    lax.fori_loop(early, basis_ref.shape[0], generate, 0)
+    lax.fori_loop(early, basis_ref.shape[0], generate, 0, unroll=3)
     own.wait()
     drain(reports_ref, devices - 1, report_send_sem)
     drain(reports_ref, devices - 1, report_recv_sem)
@@ -353,7 +354,6 @@
 
     turned = jnp.transpose(fields, (2, 0, 1)).reshape(chan_count, pixels)
     turned = jnp.pad(turned, ((0, active * chan - chan_count), (0, 0)))
-    turned = turned.reshape(active, chan, pixels)
 
     lanes = round_up((2 * groups + 1) * row_count, 128)
     basis = basis_spectra.reshape(band_count * TAPS, basis_count, 2, freq_count)
@@ -366,18 +366,23 @@
             jax.ShapeDtypeStruct((devices, 1, lanes), jnp.float32),
             jax.ShapeDtypeStruct((band_count * TAPS, 2 * chan, bins), jnp.float32),
         ],
-        in_specs=[SMEM] * 2 + [VMEM] * 3,
+        in_specs=[SMEM] * 2 + [VMEM] * 4,
         out_specs=[VMEM] * 3,
         scratch_shapes=[
-            pltpu.VMEM((active * chan, 128), jnp.float32),
-            pltpu.VMEM((active * chan, 128), jnp.float32),
             pltpu.VMEM((1, lanes), jnp.float32),
         ]
         + [DMA] * 5,
         compiler_params=pltpu.CompilerParams(
             collective_id=0, has_side_effects=True, vmem_limit_bytes=60 * 1024 * 1024
         ),
-    )(group_size, band_of_row, turned, basis_coef.T, basis)
+    )(
+        group_size,
+        band_of_row,
+        turned.reshape(active, chan, pixels),
+        turned,
+        basis_coef.T,
+        basis,
+    )
     table, sums, weight = dft_tables(lon_count, pieces, width, bins)
     mixed = pl.pallas_call(
         functools.partial(corr_body, pieces, row_count, col_count, width, bins, groups),

time: 71.6 us -> 69.2 us (0.966)
  Pallas kernels: 54.9 us -> 52.5 us
    pallas_call x1, Pallas kernels: 29.1 us -> 25.3 us  [per_device(): pl.pallas_call(functools.partial(scatter_body, devices, active, freq_coun...]
    reshape x0 -> x2, local copies, waits for them, and re-layouts: none -> 2.6 us  [per_device(): turned = jnp.transpose(fields, (2, 0, 1)).reshape(chan_count, pixels)]
    unnamed x6 -> x4, local copies, waits for them, and re-layouts: 2.61 us -> 0.01 us
    pallas_call x1, Pallas kernels: 18.1 us -> 19.4 us  [per_device(): pl.pallas_call(functools.partial(gather_body, devices, active), out_shape...]
where the time goes in v4:
time: 69.2 us; the launch traced here: 68.8 us
  Pallas kernels  52.5 us (76%)
  matrix products  8.08 us (12%)
  local copies, waits for them, and re-layouts  5.84 us (8%)
  other arithmetic  2.38 us (3%)
    pallas_call x1, Pallas kernels, per_device(): pl.pallas_call(functools.partial(scatter_body, devices, active, freq_coun...  25.3 us
    pallas_call x1, Pallas kernels, per_device(): pl.pallas_call(functools.partial(gather_body, devices, active), out_shape...  19.4 us
    dot_general x1, matrix products, per_device(): result = inputs + jnp.dot(hidden, w_out, preferred_element_type=jnp.float32)  8.08 us
    pallas_call x1, Pallas kernels, per_device(): pl.pallas_call(functools.partial(corr_body, pieces, row_count, col_count,...  7.74 us
    reshape x2, local copies, waits for them, and re-layouts, per_device(): turned = jnp.transpose(fields, (2, 0, 1)).reshape(chan_count, pixels)  2.6 us
    reshape x2, local copies, waits for them, and re-layouts, per_device(): return result.astype(jnp.bfloat16).reshape(row_count, col_count, chan_count)  2.39 us

profile of v4, /device:TPU:0, one launch (start us, length us, event | category | flops | bytes accessed | tf_op | source)
XLA Modules:
  0.0 68.8 jit_solution(4799968776704455884)
XLA Ops:
  0.0 0.0 copy-start
  0.0 1.9 %copy.18 = bf16[641,4,90]{2,1,0:T(4,128)(2,1)S(1)} copy(bf16[641,4,90]{0,1,2:T(4,128)(2,1)} %bitcast.35) | data formatting | bytes 923040 | tf_op jit(solution)/shard_map/reshape | solution.py:355
  2.0 0.7 reshape.33
  2.6 0.8 %pad.4.flat_ref = bf16[648,360]{1,0:T(8,128)(2,1)} pad(bf16[641,360]{1,0:T(8,128)(2,1)S(1)} %reshape.33, bf16[]{:T(256)} %constant.36.clone.1), padding=0_7x0_0 | pad | bytes 928082 | tf_op jit(solution)/shard_map/jit(_pad)/pad | solution.py:356
  3.5 25.3 %shard_map.109 = (bf16[32,24,360]{2,1,0:T(8,128)(2,1)}, f32[32,1,128]{2,1,0:T(1,128)}, f32[72,48,384]{2,1,0:T(8,128)}) custom-call(s32[8]{0:T(128)} %size_ref.3, s32[4]{0:T(128)} %band_ref.1, bf16[27,24,360]{2,1,0:T(8,128)(2,1)} %bitcast.33, bf16[648,360]{1,0:T(8,128)(2,1)} %pad.4.flat_ref, f32[8,641]{1,0:T(8,128)} %bitcast.36, f32[72,8,2,361]{3,2,1,0:T(2,128)} %bitcast.34), custom_call_target="tpu_custom_call" | custom-call | tf_op jit(solution)/shard_map/pallas_call | solution.py:360
  28.8 7.7 %shard_map.110.mixed_ref = bf16[32,24,360]{2,1,0:T(8,128)(2,1)} custom-call(s32[8]{0:T(128)} %size_ref.3, bf16[32,24,360]{2,1,0:T(8,128)(2,1)} %get-tuple-element.8.block_ref, f32[32,1,128]{2,1,0:T(1,128)} %get-tuple-element.9.reports_ref, bf16[1024,768]{1,0:T(8,128)(2,1)} %constant.76.clone.table_ref, f32[1,768]{1,0:T(1,128)} %constant.77.clone.total_ref, ...), custom_call_target="tpu_custom_call" | custom-call | tf_op jit(solution)/shard_map/pallas_call | solution.py:387
  36.5 0.0 copy-start.1
  36.5 19.4 %shard_map.111 = bf16[27,24,360]{2,1,0:T(8,128)(2,1)} custom-call(bf16[32,24,360]{2,1,0:T(8,128)(2,1)} %shard_map.110.mixed_ref), custom_call_target="tpu_custom_call" | custom-call | tf_op jit(solution)/shard_map/pallas_call | solution.py:400
  55.9 1.2 %convert_reduce_fusion = f32[360]{0:T(512)S(1)} fusion(bf16[648,360]{1,0:T(8,128)(2,1)} %bitcast.30), kind=kLoop, calls=%fused_computation.21 | loop fusion | flops 461160 | bytes 462960 | tf_op jit(solution)/shard_map/reduce_sum | solution.py:411
  57.1 1.2 %fusion.14 = f32[360]{0:T(512)S(1)} fusion(f32[360]{0:T(512)S(1)} %broadcast_multiply_fusion, bf16[648,360]{1,0:T(8,128)(2,1)} %bitcast.31), kind=kLoop, calls=%fused_computation.26 | loop fusion | flops 922680 | bytes 464400 | tf_op jit(solution)/shard_map/reduce_sum | solution.py:412
  58.3 0.0 copy-done
  58.3 0.0 copy-done.1
  58.3 8.1 %fusion.10 = bf16[360,641]{0,1:T(8,128)(2,1)S(1)} fusion(bf16[1282,641]{0,1:T(8,128)(2,1)S(1)} %copy-done, bf16[641,1282]{1,0:T(8,128)(2,1)} %param.17, f32[641]{0:T(1024)S(1)} %copy-done.1, f32[360]{0:T(512)S(1)} %add_rsqrt_fusion, f32[360]{0:T(512)S(1)} %broadcast_multiply_fusion, bf16[648,360]{1,0:T(8,128)(2,1)} %bitcast.32), kind=kOutput, calls=%fused_computation.20 | convolution fusion | flops 1215181056 | bytes 4930584 | tf_op jit(solution)/shard_map/dot_general | solution.py:417
  66.4 0.8 %reshape.34 = bf16[4,90,641]{1,0,2:T(4,128)(2,1)S(1)} reshape(bf16[360,641]{0,1:T(8,128)(2,1)S(1)} %fusion.10) | data formatting | bytes 923040 | tf_op jit(solution)/shard_map/reshape | solution.py:418
  67.3 1.6 %copy.17 = bf16[4,90,641]{2,0,1:T(4,128)(2,1)} copy(bf16[4,90,641]{1,0,2:T(4,128)(2,1)S(1)} %reshape.34) | data formatting | bytes 923040 | tf_op jit(solution)/shard_map/reshape | solution.py:418
  (2 shorter events, 0.0 us)
Async XLA Ops:
  0.0 58.3 %copy-start = (bf16[1282,641]{0,1:T(8,128)(2,1)S(1)}, bf16[1282,641]{0,1:T(8,128)(2,1)}, u32[]{:S(2)}) copy-start(bf16[1282,641]{0,1:T(8,128)(2,1)} %param.18) | copy-start | bytes 4930576
  36.5 21.8 %copy-start.1 = (f32[641]{0:T(1024)S(1)}, f32[641]{0:T(1024)}, u32[]{:S(2)}) copy-start(f32[641]{0:T(1024)} %param.16) | copy-start | bytes 7696
